TPU v7x, 32 devices: a whole 2x2x4 slice. The times are simulated.
32 devices in a mesh: dp: 2 (over y), rows: 4 (over x, core), cols: 4 (over z).
Axes of the slice: x: 2, y: 2, z: 4, core: 2. Of those that a mesh axis runs over, the one named last changes fastest.
Arguments:
- tokens: bfloat16 [960, 8192], P('rows', ('dp', 'cols')), may hold values from -6 to 6
- query_weight: bfloat16 [2, 960, 960], P(None, 'rows', 'cols'), may hold values from -0.1875 to 0.1875
- key_weight: bfloat16 [2, 960, 320], P(None, 'rows', 'cols'), may hold values from -0.1875 to 0.1875
- value_weight: bfloat16 [2, 960, 320], P(None, 'rows', 'cols'), may hold values from -0.1875 to 0.1875
- out_weight: bfloat16 [2, 960, 960], P(None, 'cols', 'rows'), may hold values from -1.25 to 1.25
- gate_weight: bfloat16 [2, 960, 2560], P(None, 'rows', 'cols'), may hold values from -0.1875 to 0.1875
- up_weight: bfloat16 [2, 960, 2560], P(None, 'rows', 'cols'), may hold values from -0.1875 to 0.1875
- down_weight: bfloat16 [2, 960, 2560], P(None, 'rows', 'cols'), may hold values from -0.125 to 0.125
- attention_gain: float32 [2, 960], replicated, may hold values from 0.5 to 1.5
- feedforward_gain: float32 [2, 960], replicated, may hold values from 0.5 to 1.5
- positions: int32 [8, 1024], P('dp'), may hold values from 0 to 2047, as said below
- segments: int32 [8, 1024], P('dp'), may hold values from 0 to 2, as said below
- cotangent: bfloat16 [960, 8192], P('rows', ('dp', 'cols')), may hold values from -6 to 6
Outputs:
- layer_out: float32 [960, 8192], P('rows', ('dp', 'cols'))
- input_grad: float32 [960, 8192], P('rows', ('dp', 'cols'))
- query_grad: float32 [2, 960, 960], P(None, 'rows', 'cols')
- key_grad: float32 [2, 960, 320], P(None, 'rows', 'cols')
- value_grad: float32 [2, 960, 320], P(None, 'rows', 'cols')
- out_grad: float32 [2, 960, 960], P(None, 'cols', 'rows')
- gate_grad: float32 [2, 960, 2560], P(None, 'rows', 'cols')
- up_grad: float32 [2, 960, 2560], P(None, 'rows', 'cols')
- down_grad: float32 [2, 960, 2560], P(None, 'rows', 'cols')
- attention_gain_grad: float32 [2, 960], replicated
- feedforward_gain_grad: float32 [2, 960], replicated
Inputs may be any that keep to these rules, and one draw needn't show every extreme that they name: Along a sequence the segment numbers never fall, and every sequence holds three segments. `positions`: A position counts from its document's first token; a sequence's first document may have begun before the sequence.
All inputs are finite; a program needn't handle non-finite values.
Results may differ from a plain program's by a relative error of at most 0.03.
Values may be sent and summed in bfloat16 or wider, within the bound.
No kernel may reach another device: no remote copies, remote signals or barrier semaphores. Data moves between devices by JAX's collectives and lax.ppermute only.
A program may use at most 192 MiB of HBM per device.

v0:
```python
import jax
import jax.numpy as jnp
from jax import lax
from jax.sharding import PartitionSpec as P

HEADS = 15
KV_HEADS = 5
HEAD = 64
SEQ = 1024


EPSILON = 1e-05
NEG_FILL = -1e30
ROPE_BASE = 100000.0


def rope_tables(positions):
    half_dim = HEAD // 2
    frequency = ROPE_BASE ** (-2.0 * jnp.arange(half_dim, dtype=jnp.float32) / HEAD)
    phase_angle = positions.astype(jnp.float32)[:, None] * frequency[None, :]
    return (jnp.cos(phase_angle)[:, None, :], jnp.sin(phase_angle)[:, None, :])


def rotate(values, cosine, sine_part):
    half_dim = values.shape[-1] // 2
    lower_half = values[..., :half_dim]
    upper_half = values[..., half_dim:]
    return jnp.concatenate(
        [
            lower_half * cosine - upper_half * sine_part,
            upper_half * cosine + lower_half * sine_part,
        ],
        -1,
    )


def contract(left, right, left_dim, right_dim):
    return lax.dot_general(
        left, right, (((left_dim,), (right_dim,)), ((), ())), preferred_element_type=jnp.float32
    )


def rows_total(partial_term, share):
    return lax.psum_scatter(
        partial_term(jnp.int32(0), lax.axis_size("rows") * share),
        "rows",
        scatter_dimension=0,
        tiled=True,
    )


def cols_total(partial_term, share):
    return lax.psum_scatter(
        partial_term(jnp.int32(0), share * lax.axis_size("cols")).astype(jnp.bfloat16),
        "cols",
        scatter_dimension=0,
        tiled=True,
    ).astype(jnp.float32)


def token_project(operand, weight, flipped):
    gathered = lax.all_gather(operand, "cols", axis=0, tiled=True)
    weight_dim = 1 if flipped else 0

    def partial_term(row_start, row_count):
        return contract(gathered, weight, 1, weight_dim)

    return (rows_total(partial_term, gathered.shape[0] // lax.axis_size("rows")), gathered)


def feature_project(operand, weight, flipped):
    gathered = lax.all_gather(operand, "rows", axis=0, tiled=True)
    weight_dim = 1 if flipped else 0

    def partial_term(row_start, row_count):
        return contract(gathered, weight, 1, weight_dim)

    return (cols_total(partial_term, gathered.shape[0] // lax.axis_size("cols")), gathered)


def to_query_blocks(values):
    return lax.all_to_all(values, "cols", split_axis=0, concat_axis=1, tiled=True)


def to_head_blocks(values):
    return lax.all_to_all(values, "cols", split_axis=1, concat_axis=0, tiled=True)


def row_feature_sum(values):
    return lax.psum(values, "rows")


def norm_forward(residual, gain_part):
    feature_total = residual.shape[1] * lax.axis_size("rows")
    squares = row_feature_sum(jnp.sum(residual * residual, 1))
    inv_rms = lax.rsqrt(squares / feature_total + EPSILON)
    return ((residual * inv_rms[:, None] * gain_part[None, :]).astype(jnp.bfloat16), inv_rms)


def norm_backward(grad_normed, residual, inv_rms, gain_part):
    feature_total = residual.shape[1] * lax.axis_size("rows")
    weighted = grad_normed * gain_part[None, :]
    summed = row_feature_sum(jnp.sum(weighted * residual, 1))
    grad_residual = (
        weighted * inv_rms[:, None] - residual * (inv_rms**3 * summed / feature_total)[:, None]
    )
    gain_grad = jnp.sum(grad_normed * residual * inv_rms[:, None], 0)
    return (grad_residual, gain_grad)


def silu_backward(grad_act, gate_val, up_val):
    sigmoid_val = jax.nn.sigmoid(gate_val)
    grad_gate = grad_act * up_val * sigmoid_val * (1.0 + gate_val * (1.0 - sigmoid_val))
    grad_up = grad_act * gate_val * sigmoid_val
    return (grad_gate.astype(jnp.bfloat16), grad_up.astype(jnp.bfloat16))


def attend_forward(queries, keys, values, allowed):

    def one_group(items):
        query_set, key_set, value_set = items
        scores = jnp.einsum("gqd,kd->gqk", query_set, key_set, preferred_element_type=jnp.float32)
        scores = jnp.where(allowed[None], scores, NEG_FILL)
        peak = jnp.max(scores, -1, keepdims=True)
        weights_exp = jnp.exp(scores - peak)
        denominator = jnp.sum(weights_exp, -1, keepdims=True)
        probs = (weights_exp / denominator).astype(jnp.bfloat16)
        mixed = jnp.einsum("gqk,kd->gqd", probs, value_set, preferred_element_type=jnp.float32)
        return (mixed, peak[..., 0] + jnp.log(denominator[..., 0]))

    return lax.map(one_group, (queries, keys, values))


def attend_backward(queries, keys, values, log_norm, grad_heads, allowed):

    def one_group(items):
        query_set, key_set, value_set, log_set, grad_set = items
        scores = jnp.einsum("gqd,kd->gqk", query_set, key_set, preferred_element_type=jnp.float32)
        scores = jnp.where(allowed[None], scores, NEG_FILL)
        probs = jnp.exp(scores - log_set[..., None])
        grad_probs = jnp.einsum(
            "gqd,kd->gqk", grad_set, value_set, preferred_element_type=jnp.float32
        )
        inner = jnp.sum(probs * grad_probs, -1, keepdims=True)
        grad_scores = (probs * (grad_probs - inner)).astype(jnp.bfloat16)
        grad_query = jnp.einsum(
            "gqk,kd->gqd", grad_scores, key_set, preferred_element_type=jnp.float32
        )
        grad_key = jnp.einsum(
            "gqk,gqd->kd", grad_scores, query_set, preferred_element_type=jnp.float32
        )
        grad_value = jnp.einsum(
            "gqk,gqd->kd", probs.astype(jnp.bfloat16), grad_set, preferred_element_type=jnp.float32
        )
        return (grad_query, grad_key, grad_value)

    return lax.map(one_group, (queries, keys, values, log_norm, grad_heads))


def ffn_forward_acts(normed, gate_block, up_block, down_block):
    hidden_cols = gate_block.shape[1]
    gate_up, normed_whole = token_project(normed, jnp.concatenate([gate_block, up_block], 1), False)
    gate_val = gate_up[:, :hidden_cols]
    up_val = gate_up[:, hidden_cols:]
    activated = (gate_val * jax.nn.sigmoid(gate_val) * up_val).astype(jnp.bfloat16)
    ffn_out, act_whole = feature_project(activated, down_block, True)
    return (ffn_out, (normed_whole, gate_val, up_val, act_whole))


def ffn_backward_acts(grad_out, gate_block, up_block, down_block, kept):
    normed_whole, gate_val, up_val, act_whole = kept
    hidden_cols = gate_block.shape[1]
    grad_act, grad_whole = token_project(grad_out.astype(jnp.bfloat16), down_block, False)
    down_grad = contract(grad_whole, act_whole, 0, 0)
    grad_gate, grad_up = silu_backward(grad_act, gate_val, up_val)
    grad_joint = jnp.concatenate([grad_gate, grad_up], 1)
    grad_normed, joint_whole = feature_project(
        grad_joint, jnp.concatenate([gate_block, up_block], 1), True
    )
    joint_grad = contract(normed_whole, joint_whole, 0, 0)
    return (grad_normed, joint_grad[:, :hidden_cols], joint_grad[:, hidden_cols:], down_grad)


def on_device(
    tokens,
    query_weight,
    key_weight,
    value_weight,
    out_weight,
    gate_weight,
    up_weight,
    down_weight,
    attention_gain,
    feedforward_gain,
    positions,
    segments,
    cotangent,
):
    row_index = lax.axis_index("rows")
    col_index = lax.axis_index("cols")
    feat_width, col_tokens = tokens.shape
    block_tokens = col_tokens // lax.axis_size("rows")
    row_tokens = block_tokens * lax.axis_size("cols")
    query_width = query_weight.shape[2]
    kv_width = key_weight.shape[2]
    layer_total = query_weight.shape[0]
    groups = HEADS // KV_HEADS
    head_scale = HEAD ** (-0.5)
    flat_positions = positions.reshape(-1)
    flat_segments = segments.reshape(-1)
    key_start = row_index * row_tokens
    query_start = key_start + col_index * block_tokens
    key_place = key_start + jnp.arange(row_tokens, dtype=jnp.int32)
    query_place = query_start + jnp.arange(block_tokens, dtype=jnp.int32)
    key_segment = lax.dynamic_slice_in_dim(flat_segments, key_start, row_tokens)
    query_segment = lax.dynamic_slice_in_dim(flat_segments, query_start, block_tokens)
    allowed = (
        (key_place[None, :] <= query_place[:, None])
        & (key_place[None, :] // SEQ == query_place[:, None] // SEQ)
        & (key_segment[None, :] == query_segment[:, None])
    )
    key_cos, key_sin = rope_tables(lax.dynamic_slice_in_dim(flat_positions, key_start, row_tokens))
    query_cos, query_sin = rope_tables(
        lax.dynamic_slice_in_dim(flat_positions, query_start, block_tokens)
    )
    residual = tokens.T.astype(jnp.float32)
    saved = []
    for layer_idx in range(layer_total):
        mixer_part = lax.dynamic_slice_in_dim(
            attention_gain[layer_idx], row_index * feat_width, feat_width
        )
        ffn_part = lax.dynamic_slice_in_dim(
            feedforward_gain[layer_idx], row_index * feat_width, feat_width
        )
        joint_weight = jnp.concatenate(
            [query_weight[layer_idx], key_weight[layer_idx], value_weight[layer_idx]], 1
        )
        normed, mixer_scale = norm_forward(residual, mixer_part)
        projected, normed_whole = token_project(normed, joint_weight, False)
        projected = projected.astype(jnp.bfloat16)
        query_full = to_query_blocks(projected[:, :query_width])
        keys_full, values_full = (
            lax.all_gather(
                projected[:, query_width : query_width + kv_width], "cols", axis=1, tiled=True
            ),
            lax.all_gather(projected[:, query_width + kv_width :], "cols", axis=1, tiled=True),
        )
        queries = (
            rotate(
                query_full.astype(jnp.float32).reshape(block_tokens, HEADS, HEAD),
                query_cos,
                query_sin,
            )
            * head_scale
        ).astype(jnp.bfloat16)
        queries = queries.reshape(block_tokens, KV_HEADS, groups, HEAD).transpose(1, 2, 0, 3)
        keys_rot = (
            rotate(
                keys_full.astype(jnp.float32).reshape(row_tokens, KV_HEADS, HEAD), key_cos, key_sin
            )
            .astype(jnp.bfloat16)
            .transpose(1, 0, 2)
        )
        values_heads = values_full.reshape(row_tokens, KV_HEADS, HEAD).transpose(1, 0, 2)
        mixed, log_norm = attend_forward(queries, keys_rot, values_heads, allowed)
        mixed_low = (
            mixed.transpose(2, 0, 1, 3).reshape(block_tokens, HEADS * HEAD).astype(jnp.bfloat16)
        )
        head_part = to_head_blocks(mixed_low)
        mixer_out, head_whole = feature_project(head_part, out_weight[layer_idx], False)
        hidden_state = residual + mixer_out
        ffn_normed, ffn_scale = norm_forward(hidden_state, ffn_part)
        ffn_out, ffn_kept = ffn_forward_acts(
            ffn_normed, gate_weight[layer_idx], up_weight[layer_idx], down_weight[layer_idx]
        )
        saved.append(
            (
                residual,
                mixer_scale,
                normed_whole,
                queries,
                keys_rot,
                values_heads,
                log_norm,
                head_whole,
                hidden_state,
                ffn_scale,
                ffn_kept,
                joint_weight,
                mixer_part,
                ffn_part,
            )
        )
        residual = hidden_state + ffn_out
    query_grads = [None] * layer_total
    key_grads = [None] * layer_total
    value_grads = [None] * layer_total
    out_grads = [None] * layer_total
    gate_grads = [None] * layer_total
    up_grads = [None] * layer_total
    down_grads = [None] * layer_total
    gain_grads = [None] * layer_total
    grad_state = cotangent.T.astype(jnp.float32)
    for layer_idx in reversed(range(layer_total)):
        (
            layer_input,
            mixer_scale,
            normed_whole,
            queries,
            keys_rot,
            values_heads,
            log_norm,
            head_whole,
            hidden_state,
            ffn_scale,
            ffn_kept,
            joint_weight,
            mixer_part,
            ffn_part,
        ) = saved[layer_idx]
        grad_ffn_normed, gate_grad, up_grad, down_grad = ffn_backward_acts(
            grad_state,
            gate_weight[layer_idx],
            up_weight[layer_idx],
            down_weight[layer_idx],
            ffn_kept,
        )
        ffn_norm_grad, ffn_gain_grad = norm_backward(
            grad_ffn_normed, hidden_state, ffn_scale, ffn_part
        )
        grad_hidden = grad_state + ffn_norm_grad
        grad_mixed, mixer_grad_whole = token_project(
            grad_hidden.astype(jnp.bfloat16), out_weight[layer_idx], True
        )
        out_grads[layer_idx] = contract(head_whole, mixer_grad_whole, 0, 0)
        grad_heads = to_query_blocks(grad_mixed.astype(jnp.bfloat16))
        grad_heads = grad_heads.reshape(block_tokens, KV_HEADS, groups, HEAD).transpose(1, 2, 0, 3)
        grad_query, grad_key, grad_value = attend_backward(
            queries, keys_rot, values_heads, log_norm, grad_heads, allowed
        )
        grad_query = (
            rotate(
                grad_query.transpose(2, 0, 1, 3).reshape(block_tokens, HEADS, HEAD),
                query_cos,
                -query_sin,
            )
            * head_scale
        )
        query_part = to_head_blocks(
            grad_query.reshape(block_tokens, HEADS * HEAD).astype(jnp.bfloat16)
        )
        grad_key = rotate(grad_key.transpose(1, 0, 2), key_cos, -key_sin).reshape(
            row_tokens, KV_HEADS * HEAD
        )
        grad_value = grad_value.transpose(1, 0, 2).reshape(row_tokens, KV_HEADS * HEAD)
        key_part, value_part = (
            lax.psum_scatter(
                grad_key.astype(jnp.bfloat16), "cols", scatter_dimension=1, tiled=True
            ).astype(jnp.float32),
            lax.psum_scatter(
                grad_value.astype(jnp.bfloat16), "cols", scatter_dimension=1, tiled=True
            ).astype(jnp.float32),
        )
        grad_joint = jnp.concatenate(
            [query_part, key_part.astype(jnp.bfloat16), value_part.astype(jnp.bfloat16)], 1
        )
        grad_normed, joint_whole = feature_project(grad_joint, joint_weight, True)
        joint_grad = contract(normed_whole, joint_whole, 0, 0)
        mixer_norm_grad, mixer_gain_grad = norm_backward(
            grad_normed, layer_input, mixer_scale, mixer_part
        )
        grad_state = grad_hidden + mixer_norm_grad
        query_grads[layer_idx] = joint_grad[:, :query_width]
        key_grads[layer_idx] = joint_grad[:, query_width : query_width + kv_width]
        value_grads[layer_idx] = joint_grad[:, query_width + kv_width :]
        gate_grads[layer_idx] = gate_grad
        up_grads[layer_idx] = up_grad
        down_grads[layer_idx] = down_grad
        gain_grads[layer_idx] = jnp.stack([mixer_gain_grad, ffn_gain_grad])
    gain_padded = lax.dynamic_update_slice_in_dim(
        jnp.zeros((layer_total, 2, feat_width * lax.axis_size("rows")), jnp.float32),
        jnp.stack(gain_grads),
        row_index * feat_width,
        2,
    )
    gain_total = lax.psum(gain_padded, ("dp", "rows", "cols"))
    query_total, key_total, value_total, out_total, gate_total, up_total, down_total = (
        lax.psum(jnp.stack(query_grads).astype(jnp.bfloat16), "dp").astype(jnp.float32),
        lax.psum(jnp.stack(key_grads).astype(jnp.bfloat16), "dp").astype(jnp.float32),
        lax.psum(jnp.stack(value_grads).astype(jnp.bfloat16), "dp").astype(jnp.float32),
        lax.psum(jnp.stack(out_grads).astype(jnp.bfloat16), "dp").astype(jnp.float32),
        lax.psum(jnp.stack(gate_grads).astype(jnp.bfloat16), "dp").astype(jnp.float32),
        lax.psum(jnp.stack(up_grads).astype(jnp.bfloat16), "dp").astype(jnp.float32),
        lax.psum(jnp.stack(down_grads).astype(jnp.bfloat16), "dp").astype(jnp.float32),
    )
    return (
        residual.T,
        grad_state.T,
        query_total,
        key_total,
        value_total,
        out_total,
        gate_total,
        up_total,
        down_total,
        gain_total[:, 0],
        gain_total[:, 1],
    )


def solution(mesh):
    return jax.shard_map(
        on_device,
        mesh=mesh,
        in_specs=(
            P("rows", ("dp", "cols")),
            P(None, "rows", "cols"),
            P(None, "rows", "cols"),
            P(None, "rows", "cols"),
            P(None, "cols", "rows"),
            P(None, "rows", "cols"),
            P(None, "rows", "cols"),
            P(None, "rows", "cols"),
            P(),
            P(),
            P("dp", None),
            P("dp", None),
            P("rows", ("dp", "cols")),
        ),
        out_specs=(
            P("rows", ("dp", "cols")),
            P("rows", ("dp", "cols")),
            P(None, "rows", "cols"),
            P(None, "rows", "cols"),
            P(None, "rows", "cols"),
            P(None, "cols", "rows"),
            P(None, "rows", "cols"),
            P(None, "rows", "cols"),
            P(None, "rows", "cols"),
            P(),
            P(),
        ),
        check_vma=False,
    )
```

profile of v0, /device:TPU:0, one launch (start us, length us, event | category | flops | bytes accessed | tf_op | source)
XLA Modules:
  0.0 2383.4 jit_solution(13476231329866949247)
XLA Ops:
  24.2 40.1 %all-gather.17.cloned.1.call-done = bf16[4096,240]{0,1:T(8,128)(2,1)} async-done(((bf16[1024,240]{0,1:T(8,128)(2,1)}), bf16[4096,240]{0,1:T(8,128)(2,1)}) %all-gather.17.cloned.1.call-update) | async-done | bytes 1966096 | tf_op jit(solution)/shard_map/all_gather | solution.py:62
  73.3 54.9 %reduce-scatter.21.cloned.1.call-done = f32[1024,400]{0,1:T(8,128)} async-done(((f32[4096,400]{0,1:T(8,128)}), f32[1024,400]{0,1:T(8,128)}) %reduce-scatter.21.cloned.1.call-update) | async-done | bytes 1638416 | tf_op jit(solution)/shard_map/reduce_scatter | solution.py:44
  135.3 25.6 %all_gather.61 = bf16[1024,320]{0,1:T(8,128)(2,1)S(1)} all-gather(bf16[1024,80]{0,1:T(8,128)(2,1)S(1)} %get-tuple-element.542), channel_id=1, replica_groups=mesh['dp'=2,'rows'=4,'cols'=4] {'cols'}, dimensions={1}, use_global_device_ids=true | all-gather | bytes 819200 | tf_op jit(solution)/shard_map/all_gather | solution.py:243
  161.3 15.9 all_gather.62
  178.4 18.4 while.56
  196.8 14.7 all_to_all.122
  212.5 20.4 all-gather.19.cloned.1.call-done
  237.2 41.0 %reduce-scatter.23.cloned.1.call-done = bf16[1024,240]{0,1:T(8,128)(2,1)} async-done(((bf16[4096,240]{0,1:T(8,128)(2,1)}), bf16[1024,240]{0,1:T(8,128)(2,1)}) %reduce-scatter.23.cloned.1.call-update) | async-done | bytes 491536 | tf_op jit(solution)/shard_map/reduce_scatter | solution.py:53
  288.7 41.5 %all-gather.21.cloned.1.call-done = bf16[4096,240]{0,1:T(8,128)(2,1)} async-done(((bf16[1024,240]{0,1:T(8,128)(2,1)}), bf16[4096,240]{0,1:T(8,128)(2,1)}) %all-gather.21.cloned.1.call-update) | async-done | bytes 1966096 | tf_op jit(solution)/shard_map/all_gather | solution.py:62
  342.1 149.2 %reduce-scatter.25.cloned.1.call-done = f32[1024,1280]{1,0:T(8,128)} async-done(((f32[4096,1280]{1,0:T(8,128)}), f32[1024,1280]{1,0:T(8,128)}) %reduce-scatter.25.cloned.1.call-update) | async-done | bytes 5242896 | tf_op jit(solution)/shard_map/reduce_scatter | solution.py:44
  495.7 40.5 %all-gather.23.cloned.1.call-done = bf16[4096,640]{1,0:T(8,128)(2,1)} async-done(((bf16[1024,640]{1,0:T(8,128)(2,1)}), bf16[4096,640]{1,0:T(8,128)(2,1)}) %all-gather.23.cloned.1.call-update) | async-done | bytes 5242896 | tf_op jit(solution)/shard_map/all_gather | solution.py:72
  542.7 40.9 %reduce-scatter.27.cloned.1.call-done = bf16[1024,240]{0,1:T(8,128)(2,1)} async-done(((bf16[4096,240]{0,1:T(8,128)(2,1)}), bf16[1024,240]{0,1:T(8,128)(2,1)}) %reduce-scatter.27.cloned.1.call-update) | async-done | bytes 491536 | tf_op jit(solution)/shard_map/reduce_scatter | solution.py:53
  592.3 42.2 %all-gather.25.cloned.1.call-done = bf16[4096,240]{0,1:T(8,128)(2,1)} async-done(((bf16[1024,240]{0,1:T(8,128)(2,1)}), bf16[4096,240]{0,1:T(8,128)(2,1)}) %all-gather.25.cloned.1.call-update) | async-done | bytes 1966096 | tf_op jit(solution)/shard_map/all_gather | solution.py:62
  640.0 58.5 %reduce-scatter.29.cloned.1.call-done = f32[1024,400]{0,1:T(8,128)} async-done(((f32[4096,400]{0,1:T(8,128)}), f32[1024,400]{0,1:T(8,128)}) %reduce-scatter.29.cloned.1.call-update) | async-done | bytes 1638416 | tf_op jit(solution)/shard_map/reduce_scatter | solution.py:44
  706.2 25.6 %all_gather.67 = bf16[1024,320]{0,1:T(8,128)(2,1)S(1)} all-gather(bf16[1024,80]{0,1:T(8,128)(2,1)S(1)} %get-tuple-element.540), channel_id=1, replica_groups=mesh['dp'=2,'rows'=4,'cols'=4] {'cols'}, dimensions={1}, use_global_device_ids=true | all-gather | bytes 819200 | tf_op jit(solution)/shard_map/all_gather | solution.py:243
  732.8 15.9 all_gather.68
  749.7 14.9 while.57
  764.6 14.7 all_to_all.123
  780.3 20.4 all-gather.27.cloned.1.call-done
  805.8 40.2 %reduce-scatter.31.cloned.1.call-done = bf16[1024,240]{0,1:T(8,128)(2,1)} async-done(((bf16[4096,240]{0,1:T(8,128)(2,1)}), bf16[1024,240]{0,1:T(8,128)(2,1)}) %reduce-scatter.31.cloned.1.call-update) | async-done | bytes 491536 | tf_op jit(solution)/shard_map/reduce_scatter | solution.py:53
  855.4 34.8 %all-gather.33.cloned.1.call-done = bf16[4096,240]{0,1:T(8,128)(2,1)} async-done(((bf16[1024,240]{0,1:T(8,128)(2,1)}), bf16[4096,240]{0,1:T(8,128)(2,1)}) %all-gather.33.cloned.1.call-update) | async-done | bytes 1966096 | tf_op jit(solution)/shard_map/all_gather | solution.py:62
  898.0 36.5 %all-gather.29.cloned.1.call-done = bf16[4096,240]{0,1:T(8,128)(2,1)} async-done(((bf16[1024,240]{0,1:T(8,128)(2,1)}), bf16[4096,240]{0,1:T(8,128)(2,1)}) %all-gather.29.cloned.1.call-update) | async-done | bytes 1966096 | tf_op jit(solution)/shard_map/all_gather | solution.py:62
  934.6 16.3 fusion.147
  951.0 69.3 %reduce-scatter.37.cloned.1.call-done = f32[1024,640]{1,0:T(8,128)} async-done(((f32[4096,640]{1,0:T(8,128)}), f32[1024,640]{1,0:T(8,128)}) %reduce-scatter.37.cloned.1.call-update) | async-done | bytes 2621456 | tf_op jit(solution)/shard_map/reduce_scatter | solution.py:44
  1020.3 153.0 %reduce-scatter.33.cloned.1.call-done = f32[1024,1280]{1,0:T(8,128)} async-done(((f32[4096,1280]{1,0:T(8,128)}), f32[1024,1280]{1,0:T(8,128)}) %reduce-scatter.33.cloned.1.call-update) | async-done | bytes 5242896 | tf_op jit(solution)/shard_map/reduce_scatter | solution.py:44
  1179.9 70.3 %all-gather.35.cloned.1.call-done = bf16[4096,1280]{1,0:T(8,128)(2,1)} async-done(((bf16[1024,1280]{1,0:T(8,128)(2,1)}), bf16[4096,1280]{1,0:T(8,128)(2,1)}) %all-gather.35.cloned.1.call-update) | async-done | bytes 10485776 | tf_op jit(solution)/shard_map/all_gather | solution.py:72
  1258.4 41.7 %reduce-scatter.39.cloned.1.call-done = bf16[1024,240]{0,1:T(8,128)(2,1)} async-done(((bf16[4096,240]{0,1:T(8,128)(2,1)}), bf16[1024,240]{0,1:T(8,128)(2,1)}) %reduce-scatter.39.cloned.1.call-update) | async-done | bytes 491536 | tf_op jit(solution)/shard_map/reduce_scatter | solution.py:53
  1310.4 42.5 %all-gather.37.cloned.1.call-done = bf16[4096,240]{0,1:T(8,128)(2,1)} async-done(((bf16[1024,240]{0,1:T(8,128)(2,1)}), bf16[4096,240]{0,1:T(8,128)(2,1)}) %all-gather.37.cloned.1.call-update) | async-done | bytes 1966096 | tf_op jit(solution)/shard_map/all_gather | solution.py:62
  1357.1 41.7 %reduce-scatter.41.cloned.1.call-done = f32[1024,240]{0,1:T(8,128)} async-done(((f32[4096,240]{0,1:T(8,128)}), f32[1024,240]{0,1:T(8,128)}) %reduce-scatter.41.cloned.1.call-update) | async-done | bytes 983056 | tf_op jit(solution)/shard_map/reduce_scatter | solution.py:44
  1421.6 50.6 %while.58 = (s32[]{:T(128)}, f32[5,3,256,64]{2,3,1,0:T(8,128)}, f32[5,1024,64]{1,2,0:T(8,128)}, bf16[5,1024,64]{1,2,0:T(8,128)(2,1)}, bf16[5,3,256,64]{2,3,1,0:T...) while((s32[]{:T(128)}, f32[5,3,256,64]{2,3,1,0:T(8,128)}, ...), condition=%wide.region_31.32_spmd.clone, body=%wide.region_29.31_spmd.clone.sunk | while | flops 514063616 | bytes 26191008 | solution.py:157
  1475.1 25.4 %all_to_all.124 = bf16[256,4,240]{0,2,1:T(8,128)(2,1)S(1)} all-to-all(bf16[256,4,240]{0,2,1:T(8,128)(2,1)S(1)} %bitcast.471), channel_id=1, replica_groups=mesh['dp'=2,'rows'=4,'cols'=4] {'cols'}, dimensions={1} | all-to-all | bytes 983040 | tf_op jit(solution)/shard_map/all_to_all | solution.py:86
  1500.5 24.2 %reduce-scatter.43.cloned.1.call-done = bf16[1024,80]{0,1:T(8,128)(2,1)} async-done(((bf16[1024,320]{0,1:T(8,128)(2,1)}), bf16[1024,80]{0,1:T(8,128)(2,1)}) %reduce-scatter.43.cloned.1.call-update) | async-done | bytes 163856 | tf_op jit(solution)/shard_map/reduce_scatter | solution.py:357
  1527.3 27.5 %all-gather.39.cloned.1.call-done = bf16[4096,400]{0,1:T(8,128)(2,1)} async-done(((bf16[1024,400]{0,1:T(8,128)(2,1)}), bf16[4096,400]{0,1:T(8,128)(2,1)}) %all-gather.39.cloned.1.call-update) | async-done | bytes 3276816 | tf_op jit(solution)/shard_map/all_gather | solution.py:72
  1559.4 37.2 %all-gather.31.cloned.1.call-done = bf16[4096,640]{1,0:T(8,128)(2,1)} async-done(((bf16[1024,640]{1,0:T(8,128)(2,1)}), bf16[4096,640]{1,0:T(8,128)(2,1)}) %all-gather.31.cloned.1.call-update) | async-done | bytes 5242896 | tf_op jit(solution)/shard_map/all_gather | solution.py:72
  1602.4 38.2 %reduce-scatter.47.cloned.1.call-done = bf16[1024,240]{0,1:T(8,128)(2,1)} async-done(((bf16[4096,240]{0,1:T(8,128)(2,1)}), bf16[1024,240]{0,1:T(8,128)(2,1)}) %reduce-scatter.47.cloned.1.call-update) | async-done | bytes 491536 | tf_op jit(solution)/shard_map/reduce_scatter | solution.py:53
  1648.7 34.9 %reduce-scatter.35.cloned.1.call-done = bf16[1024,240]{0,1:T(8,128)(2,1)} async-done(((bf16[4096,240]{0,1:T(8,128)(2,1)}), bf16[1024,240]{0,1:T(8,128)(2,1)}) %reduce-scatter.35.cloned.1.call-update) | async-done | bytes 491536 | tf_op jit(solution)/shard_map/reduce_scatter | solution.py:53
  1686.8 42.7 %all-gather.41.cloned.1.call-done = bf16[4096,240]{0,1:T(8,128)(2,1)} async-done(((bf16[1024,240]{0,1:T(8,128)(2,1)}), bf16[4096,240]{0,1:T(8,128)(2,1)}) %all-gather.41.cloned.1.call-update) | async-done | bytes 1966096 | tf_op jit(solution)/shard_map/all_gather | solution.py:62
  1737.2 83.1 %reduce-scatter.49.cloned.1.call-done = f32[1024,640]{1,0:T(8,128)} async-done(((f32[4096,640]{1,0:T(8,128)}), f32[1024,640]{1,0:T(8,128)}) %reduce-scatter.49.cloned.1.call-update) | async-done | bytes 2621456 | tf_op jit(solution)/shard_map/reduce_scatter | solution.py:44
  1826.7 70.2 %all-gather.43.cloned.1.call-done = bf16[4096,1280]{1,0:T(8,128)(2,1)} async-done(((bf16[1024,1280]{1,0:T(8,128)(2,1)}), bf16[4096,1280]{1,0:T(8,128)(2,1)}) %all-gather.43.cloned.1.call-update) | async-done | bytes 10485776 | tf_op jit(solution)/shard_map/all_gather | solution.py:72
  1905.3 41.7 %reduce-scatter.51.cloned.1.call-done = bf16[1024,240]{0,1:T(8,128)(2,1)} async-done(((bf16[4096,240]{0,1:T(8,128)(2,1)}), bf16[1024,240]{0,1:T(8,128)(2,1)}) %reduce-scatter.51.cloned.1.call-update) | async-done | bytes 491536 | tf_op jit(solution)/shard_map/reduce_scatter | solution.py:53
  1957.5 42.5 %all-gather.45.cloned.1.call-done = bf16[4096,240]{0,1:T(8,128)(2,1)} async-done(((bf16[1024,240]{0,1:T(8,128)(2,1)}), bf16[4096,240]{0,1:T(8,128)(2,1)}) %all-gather.45.cloned.1.call-update) | async-done | bytes 1966096 | tf_op jit(solution)/shard_map/all_gather | solution.py:62
  2004.2 41.7 %reduce-scatter.53.cloned.1.call-done = f32[1024,240]{0,1:T(8,128)} async-done(((f32[4096,240]{0,1:T(8,128)}), f32[1024,240]{0,1:T(8,128)}) %reduce-scatter.53.cloned.1.call-update) | async-done | bytes 983056 | tf_op jit(solution)/shard_map/reduce_scatter | solution.py:44
  2068.5 52.8 %while.59 = (s32[]{:T(128)}, f32[5,3,256,64]{2,3,1,0:T(8,128)}, f32[5,1024,64]{1,2,0:T(8,128)}, bf16[5,1024,64]{1,2,0:T(8,128)(2,1)S(1)}, bf16[5,3,256,64]{2,3,1...) while((s32[]{:T(128)}, f32[5,3,256,64]{2,3,1,0:T(8,128)}, ...), condition=%wide.region_44.45_spmd.clone, body=%wide.region_42.44_spmd.clone.sunk | while | flops 514063616 | bytes 26193056 | solution.py:157
  2125.8 24.6 %all_to_all.125 = bf16[256,4,240]{0,2,1:T(8,128)(2,1)S(1)} all-to-all(bf16[256,4,240]{0,2,1:T(8,128)(2,1)S(1)} %bitcast.472), channel_id=1, replica_groups=mesh['dp'=2,'rows'=4,'cols'=4] {'cols'}, dimensions={1} | all-to-all | bytes 983040 | tf_op jit(solution)/shard_map/all_to_all | solution.py:86
  2150.5 23.9 %reduce-scatter.55.cloned.1.call-done = bf16[1024,80]{0,1:T(8,128)(2,1)} async-done(((bf16[1024,320]{0,1:T(8,128)(2,1)}), bf16[1024,80]{0,1:T(8,128)(2,1)}) %reduce-scatter.55.cloned.1.call-update) | async-done | bytes 163856 | tf_op jit(solution)/shard_map/reduce_scatter | solution.py:357
  2215.2 66.9 %all-reduce.3.cloned.1.call-done = (bf16[2,240,240]{1,2,0:T(8,128)(2,1)}, bf16[2,240,80]{1,2,0:T(8,128)(2,1)}, bf16[2,240,80]{1,2,0:T(8,128)(2,1)}, bf16[2,240,2...) async-done(((bf16[2,240,240]{1,2,0:T(8,128)(2,1)}, bf16[2,240,80]{1,2,0:T(8,128)(2,1)}, ...) | async-done | bytes 2457616 | tf_op jit(solution)/shard_map/psum | solution.py:388
  2293.4 32.7 %reduce-scatter.59.cloned.1.call-done = bf16[1024,240]{0,1:T(8,128)(2,1)} async-done(((bf16[4096,240]{0,1:T(8,128)(2,1)}), bf16[1024,240]{0,1:T(8,128)(2,1)}) %reduce-scatter.59.cloned.1.call-update) | async-done | bytes 491536 | tf_op jit(solution)/shard_map/reduce_scatter | solution.py:53
  2327.8 39.7 %psum.127 = f32[2,2,960]{2,0,1:T(2,128)S(1)} all-reduce(f32[2,2,960]{2,0,1:T(2,128)S(1)} %dynamic_update_slice.36), channel_id=1, replica_groups=mesh['dp'=2,'rows'=4,'cols'=4] {'dp','rows','cols'}, use_global_device_ids=true, to_apply=%region_61.62 | all-reduce | flops 3840 | bytes 30720 | tf_op jit(solution)/shard_map/psum | solution.py:386
  (587 shorter events, 461.4 us)
Async XLA Ops:
  7.2 57.0 %all-gather.17.cloned.1.call-start = ((), (), s32[]{:S(2)}) async-start(), calls=%async_computation.28 | async-start | bytes 2457600 | tf_op jit(solution)/shard_map/all_gather | solution.py:62
  20.3 107.9 %reduce-scatter.21.cloned.1.call-start = ((), (), s32[]{:S(2)}) async-start(), calls=%async_computation.29 | async-start | bytes 8192000 | tf_op jit(solution)/shard_map/reduce_scatter | solution.py:44
  130.7 46.5 %all-to-all-start = ((bf16[4,256,240]{1,2,0:T(8,128)(2,1)}), bf16[4,256,240]{1,2,0:T(8,128)(2,1)S(1)}, u32[]{:S(2)}, u32[]{:S(2)}) async-start(bf16[4,256,240]{1,2,0:T(8,128)(2,1)} %bitcast.375), calls=%async_computation.1 | async-start | bytes 983040 | tf_op jit(solution)/shard_map/all_to_all | solution.py:82
  135.3 97.6 %all-gather.19.cloned.1.call-start = ((), (), s32[]{:S(2)}) async-start(), calls=%async_computation.30 | async-start | bytes 2457600 | tf_op jit(solution)/shard_map/all_gather | solution.py:72
  212.5 65.8 %reduce-scatter.23.cloned.1.call-start = ((), (), s32[]{:S(2)}) async-start(), calls=%async_computation.31 | async-start | bytes 2457600 | tf_op jit(solution)/shard_map/reduce_scatter | solution.py:53
  236.5 93.7 %all-gather.21.cloned.1.call-start = ((), (), s32[]{:S(2)}) async-start(), calls=%async_computation.32 | async-start | bytes 2457600 | tf_op jit(solution)/shard_map/all_gather | solution.py:62
  287.7 203.6 %reduce-scatter.25.cloned.1.call-start = ((), (), s32[]{:S(2)}) async-start(), calls=%async_computation.33 | async-start | bytes 26214400 | tf_op jit(solution)/shard_map/reduce_scatter | solution.py:44
  341.8 194.4 %copy-start.37 = (bf16[2,240,640]{2,1,0:T(8,128)(2,1)S(1)}, bf16[2,240,640]{2,1,0:T(8,128)(2,1)}, u32[]{:S(2)}) copy-start(bf16[2,240,640]{2,1,0:T(8,128)(2,1)} %param.28) | copy-start | bytes 1843204
  341.8 194.4 %all-gather.23.cloned.1.call-start = ((), (), s32[]{:S(2)}) async-start(), calls=%async_computation.34 | async-start | bytes 6553600 | tf_op jit(solution)/shard_map/all_gather | solution.py:72
  495.7 87.9 %reduce-scatter.27.cloned.1.call-start = ((), (), s32[]{:S(2)}) async-start(), calls=%async_computation.35 | async-start | bytes 2457600 | tf_op jit(solution)/shard_map/reduce_scatter | solution.py:53
  541.8 92.7 %all-gather.25.cloned.1.call-start = ((), (), s32[]{:S(2)}) async-start(), calls=%async_computation.36 | async-start | bytes 2457600 | tf_op jit(solution)/shard_map/all_gather | solution.py:62
  592.0 106.5 %reduce-scatter.29.cloned.1.call-start = ((), (), s32[]{:S(2)}) async-start(), calls=%async_computation.37 | async-start | bytes 8192000 | tf_op jit(solution)/shard_map/reduce_scatter | solution.py:44
  701.6 47.0 %all-to-all-start.2 = ((bf16[4,256,240]{1,2,0:T(8,128)(2,1)}), bf16[4,256,240]{1,2,0:T(8,128)(2,1)S(1)}, u32[]{:S(2)}, u32[]{:S(2)}) async-start(bf16[4,256,240]{1,2,0:T(8,128)(2,1)} %bitcast.374), calls=%async_computation.7 | async-start | bytes 983040 | tf_op jit(solution)/shard_map/all_to_all | solution.py:82
  706.2 94.4 %all-gather.27.cloned.1.call-start = ((), (), s32[]{:S(2)}) async-start(), calls=%async_computation.38 | async-start | bytes 2457600 | tf_op jit(solution)/shard_map/all_gather | solution.py:72
  780.2 65.8 %reduce-scatter.31.cloned.1.call-start = ((), (), s32[]{:S(2)}) async-start(), calls=%async_computation.39 | async-start | bytes 2457600 | tf_op jit(solution)/shard_map/reduce_scatter | solution.py:53
  804.2 86.0 %all-gather.33.cloned.1.call-start = ((), (), s32[]{:S(2)}) async-start(), calls=%async_computation.44 | async-start | bytes 2457600 | tf_op jit(solution)/shard_map/all_gather | solution.py:62
  805.0 129.6 %all-gather.29.cloned.1.call-start = ((), (), s32[]{:S(2)}) async-start(), calls=%async_computation.40 | async-start | bytes 2457600 | tf_op jit(solution)/shard_map/all_gather | solution.py:62
  805.8 502.4 %copy-start.87 = (f32[1,240]{1,0:T(1,128)}, f32[1,240]{1,0:T(1,128)S(1)}, u32[]{:S(2)}) copy-start(f32[1,240]{1,0:T(1,128)S(1)} %constant_dynamic-slice_fusion) | copy-start | bytes 2884
  853.4 454.8 %copy-start.66 = (f32[1024]{0:T(1024)}, f32[1024]{0:T(1024)S(1)}, u32[]{:S(2)}) copy-start(f32[1024]{0:T(1024)S(1)} %add_rsqrt_fusion) | copy-start | bytes 12292
  855.4 164.9 %reduce-scatter.37.cloned.1.call-start = ((), (), s32[]{:S(2)}) async-start(), calls=%async_computation.45 | async-start | bytes 13107200 | tf_op jit(solution)/shard_map/reduce_scatter | solution.py:44
  897.5 275.7 %reduce-scatter.33.cloned.1.call-start = ((), (), s32[]{:S(2)}) async-start(), calls=%async_computation.41 | async-start | bytes 26214400 | tf_op jit(solution)/shard_map/reduce_scatter | solution.py:44
  950.9 299.2 %all-gather.35.cloned.1.call-start = ((), (), s32[]{:S(2)}) async-start(), calls=%async_computation.46 | async-start | bytes 13107200 | tf_op jit(solution)/shard_map/all_gather | solution.py:72
  1179.8 120.3 %reduce-scatter.39.cloned.1.call-start = ((), (), s32[]{:S(2)}) async-start(), calls=%async_computation.47 | async-start | bytes 2457600 | tf_op jit(solution)/shard_map/reduce_scatter | solution.py:53
  1258.4 94.6 %all-gather.37.cloned.1.call-start = ((), (), s32[]{:S(2)}) async-start(), calls=%async_computation.48 | async-start | bytes 2457600 | tf_op jit(solution)/shard_map/all_gather | solution.py:62
  1310.4 88.5 %reduce-scatter.41.cloned.1.call-start = ((), (), s32[]{:S(2)}) async-start(), calls=%async_computation.49 | async-start | bytes 4915200 | tf_op jit(solution)/shard_map/reduce_scatter | solution.py:44
  1400.9 18.3 all-to-all-start.4
  1405.6 95.0 %reduce-scatter.45.cloned.1.call-start = ((), (), s32[]{:S(2)}) async-start(), calls=%async_computation.51 | async-start | bytes 819200 | tf_op jit(solution)/shard_map/reduce_scatter | solution.py:360
  1472.2 52.5 %reduce-scatter.43.cloned.1.call-start = ((), (), s32[]{:S(2)}) async-start(), calls=%async_computation.50 | async-start | bytes 819200 | tf_op jit(solution)/shard_map/reduce_scatter | solution.py:357
  1474.8 80.0 %all-gather.39.cloned.1.call-start = ((), (), s32[]{:S(2)}) async-start(), calls=%async_computation.52 | async-start | bytes 4096000 | tf_op jit(solution)/shard_map/all_gather | solution.py:72
  1526.7 70.0 %all-gather.31.cloned.1.call-start = ((), (), s32[]{:S(2)}) async-start(), calls=%async_computation.42 | async-start | bytes 6553600 | tf_op jit(solution)/shard_map/all_gather | solution.py:72
  1527.3 113.3 %reduce-scatter.47.cloned.1.call-start = ((), (), s32[]{:S(2)}) async-start(), calls=%async_computation.53 | async-start | bytes 2457600 | tf_op jit(solution)/shard_map/reduce_scatter | solution.py:53
  1559.4 124.1 %reduce-scatter.35.cloned.1.call-start = ((), (), s32[]{:S(2)}) async-start(), calls=%async_computation.43 | async-start | bytes 2457600 | tf_op jit(solution)/shard_map/reduce_scatter | solution.py:53
  1602.4 127.1 %all-gather.41.cloned.1.call-start = ((), (), s32[]{:S(2)}) async-start(), calls=%async_computation.54 | async-start | bytes 2457600 | tf_op jit(solution)/shard_map/all_gather | solution.py:62
  1686.8 133.5 %reduce-scatter.49.cloned.1.call-start = ((), (), s32[]{:S(2)}) async-start(), calls=%async_computation.55 | async-start | bytes 13107200 | tf_op jit(solution)/shard_map/reduce_scatter | solution.py:44
  1736.9 160.0 %all-gather.43.cloned.1.call-start = ((), (), s32[]{:S(2)}) async-start(), calls=%async_computation.56 | async-start | bytes 13107200 | tf_op jit(solution)/shard_map/all_gather | solution.py:72
  1826.6 120.4 %copy-start.1 = (bf16[240,1024]{1,0:T(8,128)(2,1)S(1)}, bf16[240,1024]{1,0:T(8,128)(2,1)}, u32[]{:S(2)}) copy-start(bf16[240,1024]{1,0:T(8,128)(2,1)} %param.21) | copy-start | bytes 1474564
  1826.6 120.4 %copy-start.3 = (bf16[1024,240]{0,1:T(8,128)(2,1)S(1)}, bf16[1024,240]{0,1:T(8,128)(2,1)}, u32[]{:S(2)}) copy-start(bf16[1024,240]{0,1:T(8,128)(2,1)} %reduce-scatter.23.cloned.1.call-done) | copy-start | bytes 1474564
  1826.6 120.4 %copy-start.64 = (f32[1024]{0:T(1024)S(1)}, f32[1024]{0:T(1024)}, u32[]{:S(2)}) copy-start(f32[1024]{0:T(1024)} %copy-done.63) | copy-start | bytes 12292
  1826.6 120.4 %copy-start.85 = (f32[1,240]{1,0:T(1,128)S(1)}, f32[1,240]{1,0:T(1,128)}, u32[]{:S(2)}) copy-start(f32[1,240]{1,0:T(1,128)} %copy-done.84) | copy-start | bytes 2884
  1826.6 120.4 %reduce-scatter.51.cloned.1.call-start = ((), (), s32[]{:S(2)}) async-start(), calls=%async_computation.57 | async-start | bytes 2457600 | tf_op jit(solution)/shard_map/reduce_scatter | solution.py:53
  1905.3 94.6 %all-gather.45.cloned.1.call-start = ((), (), s32[]{:S(2)}) async-start(), calls=%async_computation.58 | async-start | bytes 2457600 | tf_op jit(solution)/shard_map/all_gather | solution.py:62
  1957.4 88.5 %reduce-scatter.53.cloned.1.call-start = ((), (), s32[]{:S(2)}) async-start(), calls=%async_computation.59 | async-start | bytes 4915200 | tf_op jit(solution)/shard_map/reduce_scatter | solution.py:44
  2048.0 18.2 all-to-all-start.6
  2052.6 97.9 %reduce-scatter.57.cloned.1.call-start = ((), (), s32[]{:S(2)}) async-start(), calls=%async_computation.61 | async-start | bytes 819200 | tf_op jit(solution)/shard_map/reduce_scatter | solution.py:360
  2122.2 52.2 %reduce-scatter.55.cloned.1.call-start = ((), (), s32[]{:S(2)}) async-start(), calls=%async_computation.60 | async-start | bytes 819200 | tf_op jit(solution)/shard_map/reduce_scatter | solution.py:357
  2124.7 79.8 %all-gather.47.cloned.1.call-start = ((), (), s32[]{:S(2)}) async-start(), calls=%async_computation.62 | async-start | bytes 4096000 | tf_op jit(solution)/shard_map/all_gather | solution.py:72
  2176.4 105.7 %all-reduce.3.cloned.1.call-start = ((), (), s32[]{:S(2)}) async-start(), calls=%async_computation.64 | async-start | bytes 4997120 | tf_op jit(solution)/shard_map/psum | solution.py:388
  2210.2 115.9 %reduce-scatter.59.cloned.1.call-start = ((), (), s32[]{:S(2)}) async-start(), calls=%async_computation.63 | async-start | bytes 2457600 | tf_op jit(solution)/shard_map/reduce_scatter | solution.py:53
  (98 other events, 3596.0 us)
Sparse Core Ops, SparseCore 0:
  20.4 43.8 all-gather.16
  69.8 58.3 reduce-scatter.20
  212.6 20.2 all-gather.18
  236.6 41.5 reduce-scatter.22
  287.8 42.3 all-gather.20
  342.0 149.3 reduce-scatter.24
  495.8 40.4 all-gather.22
  541.9 41.6 reduce-scatter.26
  592.1 42.3 all-gather.24
  640.1 58.3 reduce-scatter.28
  780.3 20.2 all-gather.26
  804.3 41.5 reduce-scatter.30
  847.6 42.6 all-gather.32
  892.2 42.3 all-gather.28
  937.0 83.2 reduce-scatter.36
  1022.7 150.4 reduce-scatter.32
  1179.9 70.1 all-gather.34
  1258.5 41.5 reduce-scatter.38
  1310.5 42.3 all-gather.36
  1357.2 41.5 reduce-scatter.40
  1472.4 27.1 reduce-scatter.44
  1502.4 22.3 reduce-scatter.42
  1526.9 27.8 all-gather.38
  1556.2 40.3 all-gather.30
  1599.0 41.5 reduce-scatter.46
  1642.8 40.6 reduce-scatter.34
  1686.9 42.5 all-gather.40
  1737.0 83.2 reduce-scatter.48
  1826.7 70.1 all-gather.42
  1905.4 41.5 reduce-scatter.50
  1957.5 42.3 all-gather.44
  2004.3 41.5 reduce-scatter.52
  2122.3 26.8 reduce-scatter.56
  2152.1 22.3 reduce-scatter.54
  2176.6 27.8 all-gather.46
  2210.3 71.7 all-reduce.2
  2284.3 41.7 reduce-scatter.58
where the time goes:
time: 2400 us; the launch traced here: 2380 us
  waiting for transfers between devices  1720 us (72%)
  blocking collectives  253 us (11%)
  matrix products  227 us (9%)
  other arithmetic  113 us (5%)
  local copies, waits for them, and re-layouts  35 us (1%)
    reduce_scatter x8, waiting for transfers between devices, rows_total(): lax.psum_scatter(partial_term(jnp.int32(0), lax.axis_size('rows') * share...  651 us
    all_gather x8, waiting for transfers between devices, token_project(): gathered = lax.all_gather(operand, 'cols', axis=0, tiled=True)  323 us
    reduce_scatter x8, waiting for transfers between devices, cols_total(): lax.psum_scatter(partial_term(jnp.int32(0), share * lax.axis_size('cols')...  311 us
    all_gather x8, waiting for transfers between devices, feature_project(): gathered = lax.all_gather(operand, 'rows', axis=0, tiled=True)  289 us
    dot_general x24, matrix products, contract(): lax.dot_general(left, right, (((left_dim,), (right_dim,)), ((), ())), pre...  128 us
    all_to_all x4, blocking collectives, to_head_blocks(): lax.all_to_all(values, 'cols', split_axis=1, concat_axis=0, tiled=True)  79.4 us
    psum x1, waiting for transfers between devices, on_device(): lax.psum(jnp.stack(query_grads).astype(jnp.bfloat16), 'dp')  66.9 us
    all_gather x2, blocking collectives, on_device(): lax.all_gather(projected[:, query_width:query_width + kv_width], 'cols',...  51.3 us
  transfers between devices with their start and end apart: 41, of which 37 were waited for; matrix products, arithmetic and copies ran while one was open for 4% of the time, Pallas kernels for 0%

commit v1 on v0

v1 whole, which is shorter than its diff:
```python
import jax
import jax.numpy as jnp
from jax import lax
from jax.sharding import PartitionSpec as P

HEADS = 15
KV_HEADS = 5
HEAD = 64
SEQ = 1024
GROUPS = HEADS // KV_HEADS
EPSILON = 1e-05
NEG_FILL = -1e30
ROPE_BASE = 100000.0
LOW = jnp.bfloat16


def contract(left, right, left_dim, right_dim):
    return lax.dot_general(
        left, right, (((left_dim,), (right_dim,)), ((), ())), preferred_element_type=jnp.float32
    )


def rope_tables(positions):
    half_dim = HEAD // 2
    frequency = ROPE_BASE ** (-2.0 * jnp.arange(half_dim, dtype=jnp.float32) / HEAD)
    angle = positions.astype(jnp.float32)[:, None] * frequency[None, :]
    return jnp.cos(angle)[:, None, :], jnp.sin(angle)[:, None, :]


def rotate(values, cosine, sine):
    rows, width = values.shape
    split = values.reshape(rows, width // HEAD, HEAD)
    lower, upper = split[..., : HEAD // 2], split[..., HEAD // 2 :]
    turned = jnp.concatenate([lower * cosine - upper * sine, upper * cosine + lower * sine], -1)
    return turned.reshape(rows, width)


def swap_rows(value, step):
    count = lax.axis_size("rows")
    return lax.ppermute(value, "rows", [(i, i ^ step) for i in range(count)])


def rows_gather(block):
    count = lax.axis_size("rows")
    blocks = {0: block}
    step = count // 2
    while step:
        held = sorted(blocks)
        got = swap_rows(jnp.concatenate([blocks[i] for i in held], 0), step)
        for n, i in enumerate(held):
            blocks[i ^ step] = got[n * block.shape[0] : (n + 1) * block.shape[0]]
        step //= 2
    return jnp.concatenate([blocks[i] for i in range(count)], 0)


def rows_scatter(partial):
    count = lax.axis_size("rows")
    size = partial.shape[0] // count
    blocks = {i: partial[i * size : (i + 1) * size] for i in range(count)}
    step = 1
    while step < count:
        kept = [i for i in sorted(blocks) if not i & step]
        sent = jnp.concatenate([blocks[i ^ step] for i in kept], 0).astype(LOW)
        got = swap_rows(sent, step)
        blocks = {
            i: blocks[i] + got[n * size : (n + 1) * size].astype(jnp.float32)
            for n, i in enumerate(kept)
        }
        step *= 2
    return blocks[0]


def rows_exchange(chunks, row_index):
    count = lax.axis_size("rows")
    own = lax.dynamic_index_in_dim(chunks, row_index, 0)
    result = lax.dynamic_update_slice_in_dim(jnp.zeros_like(chunks), own, row_index, 0)
    for step in range(1, count):
        peer = row_index ^ step
        got = swap_rows(lax.dynamic_index_in_dim(chunks, peer, 0), step)
        result = lax.dynamic_update_slice_in_dim(result, got, peer, 0)
    return result


def dp_total(value):
    if lax.axis_size("dp") == 2:
        other = lax.ppermute(value, "dp", [(0, 1), (1, 0)])
        return value.astype(jnp.float32) + other.astype(jnp.float32)
    return lax.psum(value, "dp").astype(jnp.float32)


def spread(value, parts):
    return value.reshape(value.shape[0], parts, -1).transpose(1, 0, 2)


def unspread(value):
    return value.transpose(1, 0, 2).reshape(value.shape[1], -1)


def norm_forward(residual, gain):
    inv_rms = lax.rsqrt(jnp.mean(residual * residual, 1, keepdims=True) + EPSILON)
    return (residual * inv_rms * gain[None, :]).astype(LOW), inv_rms


def norm_backward(grad_normed, residual, inv_rms, gain):
    weighted = grad_normed * gain[None, :]
    summed = jnp.mean(weighted * residual, 1, keepdims=True)
    grad_residual = weighted * inv_rms - residual * (inv_rms**3 * summed)
    return grad_residual, jnp.sum(grad_normed * residual * inv_rms, 0)


def split_queries(values):
    return values.reshape(-1, KV_HEADS, GROUPS, HEAD).transpose(1, 2, 0, 3)


def split_keys(values):
    return values.reshape(-1, KV_HEADS, HEAD).transpose(1, 0, 2)


def attend_forward(queries, keys, values, allowed):

    def one_group(items):
        query_set, key_set, value_set = items
        scores = jnp.einsum("gqd,kd->gqk", query_set, key_set, preferred_element_type=jnp.float32)
        scores = jnp.where(allowed[None], scores, NEG_FILL)
        peak = jnp.max(scores, -1, keepdims=True)
        weights_exp = jnp.exp(scores - peak)
        denominator = jnp.sum(weights_exp, -1, keepdims=True)
        probs = (weights_exp / denominator).astype(LOW)
        mixed = jnp.einsum("gqk,kd->gqd", probs, value_set, preferred_element_type=jnp.float32)
        return mixed, peak[..., 0] + jnp.log(denominator[..., 0])

    mixed, log_norm = lax.map(
        one_group, (split_queries(queries), split_keys(keys), split_keys(values))
    )
    return mixed.transpose(2, 0, 1, 3).reshape(-1, HEADS * HEAD).astype(LOW), log_norm


def attend_backward(queries, keys, values, log_norm, grad_mixed, allowed):

    def one_group(items):
        query_set, key_set, value_set, log_set, grad_set = items
        scores = jnp.einsum("gqd,kd->gqk", query_set, key_set, preferred_element_type=jnp.float32)
        scores = jnp.where(allowed[None], scores, NEG_FILL)
        probs = jnp.exp(scores - log_set[..., None])
        grad_probs = jnp.einsum(
            "gqd,kd->gqk", grad_set, value_set, preferred_element_type=jnp.float32
        )
        inner = jnp.sum(probs * grad_probs, -1, keepdims=True)
        grad_scores = (probs * (grad_probs - inner)).astype(LOW)
        grad_query = jnp.einsum(
            "gqk,kd->gqd", grad_scores, key_set, preferred_element_type=jnp.float32
        )
        grad_key = jnp.einsum(
            "gqk,gqd->kd", grad_scores, query_set, preferred_element_type=jnp.float32
        )
        grad_value = jnp.einsum(
            "gqk,gqd->kd", probs.astype(LOW), grad_set, preferred_element_type=jnp.float32
        )
        return grad_query, grad_key, grad_value

    grad_query, grad_key, grad_value = lax.map(
        one_group,
        (
            split_queries(queries),
            split_keys(keys),
            split_keys(values),
            log_norm,
            split_queries(grad_mixed),
        ),
    )
    return (
        grad_query.transpose(2, 0, 1, 3).reshape(-1, HEADS * HEAD),
        grad_key.transpose(1, 0, 2).reshape(-1, KV_HEADS * HEAD),
        grad_value.transpose(1, 0, 2).reshape(-1, KV_HEADS * HEAD),
    )


def on_device(
    tokens,
    query_weight,
    key_weight,
    value_weight,
    out_weight,
    gate_weight,
    up_weight,
    down_weight,
    attention_gain,
    feedforward_gain,
    positions,
    segments,
    cotangent,
):
    row_index = lax.axis_index("rows")
    col_index = lax.axis_index("cols")
    row_count = lax.axis_size("rows")
    col_count = lax.axis_size("cols")
    feat_width, col_tokens = tokens.shape
    block_tokens = col_tokens // row_count
    half_block = block_tokens // 2
    layer_total = query_weight.shape[0]
    query_width = query_weight.shape[2]
    kv_width = key_weight.shape[2]
    all_queries = query_width * col_count
    all_kv = kv_width * col_count
    head_scale = HEAD ** (-0.5)

    deal = []
    for j in range(row_count):
        deal += [j, 2 * row_count - 1 - j]
    undeal = [deal.index(b) for b in range(2 * row_count)]

    def reorder(values, order):
        parts = [values[..., b * half_block : (b + 1) * half_block] for b in order]
        return jnp.concatenate(parts, -1)

    def to_token_blocks(values):
        chunks = spread(reorder(values, deal), row_count)
        return rows_exchange(chunks, row_index).reshape(-1, block_tokens).T

    def to_feature_blocks(values):
        chunks = values.astype(LOW).T.reshape(row_count, feat_width, block_tokens)
        return reorder(unspread(rows_exchange(chunks, row_index)), undeal).astype(jnp.float32)

    def blocks_here(values):
        dealt = reorder(values, deal).reshape(row_count, block_tokens)
        picked = [
            lax.dynamic_index_in_dim(dealt, row_index ^ i, 0, keepdims=False)
            for i in range(row_count)
        ]
        return jnp.concatenate(picked)

    places = blocks_here(jnp.arange(col_tokens, dtype=jnp.int32))
    own_positions = blocks_here(
        lax.dynamic_index_in_dim(positions, col_index, 0, keepdims=False)
    )[:block_tokens]
    doc = blocks_here(lax.dynamic_index_in_dim(segments, col_index, 0, keepdims=False))
    allowed = (places[None, :] <= places[:block_tokens, None]) & (
        doc[None, :] == doc[:block_tokens, None]
    )
    cosine, sine = rope_tables(own_positions)

    def attention_weights(layer):
        joint = jnp.concatenate([query_weight[layer], key_weight[layer], value_weight[layer]], 1)
        wide = lax.all_gather(joint, "cols", axis=0)
        wide = jnp.concatenate(
            [
                unspread(wide[:, :, :query_width]),
                unspread(wide[:, :, query_width : query_width + kv_width]),
                unspread(wide[:, :, query_width + kv_width :]),
            ],
            1,
        )
        joint_full = lax.all_gather(wide, "rows", axis=0, tiled=True)
        out_wide = unspread(lax.all_gather(out_weight[layer].T, "cols", axis=0))
        out_full = lax.all_gather(out_wide, "rows", axis=0, tiled=True)
        return joint_full, out_full

    def ffn_weights(layer):
        stacked = jnp.stack([gate_weight[layer], up_weight[layer], down_weight[layer]])
        hidden = stacked.shape[2]
        chunks = stacked.transpose(0, 2, 1).reshape(3, row_count, hidden // row_count, feat_width)
        whole = rows_exchange(chunks.transpose(1, 0, 2, 3), row_index)
        whole = whole.transpose(1, 2, 0, 3).reshape(3, hidden // row_count, -1)
        return [lax.all_gather(whole[i], "cols", axis=0, tiled=True) for i in range(3)]

    def attention_grads(joint_grad, out_grad):
        part = lax.psum_scatter(joint_grad.astype(LOW), "rows", scatter_dimension=0, tiled=True)
        part = jnp.concatenate(
            [
                spread(part[:, :all_queries], col_count),
                spread(part[:, all_queries : all_queries + all_kv], col_count),
                spread(part[:, all_queries + all_kv :], col_count),
            ],
            2,
        )
        joint = dp_total(lax.psum_scatter(part, "cols", scatter_dimension=0))
        out = lax.psum_scatter(out_grad.astype(LOW), "rows", scatter_dimension=0, tiled=True)
        out = dp_total(lax.psum_scatter(spread(out, col_count), "cols", scatter_dimension=0)).T
        return (
            joint[:, :query_width],
            joint[:, query_width : query_width + kv_width],
            joint[:, query_width + kv_width :],
            out,
        )

    def ffn_grads(grads):
        parts = jnp.stack(
            [
                lax.psum_scatter(g.astype(LOW), "cols", scatter_dimension=0, tiled=True)
                for g in grads
            ]
        )
        hidden_part = parts.shape[1]
        chunks = parts.reshape(3, hidden_part, row_count, feat_width).transpose(2, 0, 1, 3)
        mine = rows_exchange(chunks, row_index).transpose(1, 3, 0, 2)
        return dp_total(mine.reshape(3, feat_width, row_count * hidden_part))

    attention_ws = [attention_weights(n) for n in range(layer_total)]
    ffn_ws = [ffn_weights(n) for n in range(layer_total)]

    residual = to_token_blocks(tokens).astype(jnp.float32)
    saved = []
    for layer in range(layer_total):
        joint_full, out_full = attention_ws[layer]
        gate_full, up_full, down_full = ffn_ws[layer]
        normed, mixer_scale = norm_forward(residual, attention_gain[layer])
        projected = contract(normed, joint_full, 1, 0).astype(LOW).astype(jnp.float32)
        queries = (rotate(projected[:, :all_queries], cosine, sine) * head_scale).astype(LOW)
        own_kv = jnp.concatenate(
            [
                rotate(projected[:, all_queries : all_queries + all_kv], cosine, sine),
                projected[:, all_queries + all_kv :],
            ],
            1,
        ).astype(LOW)
        both = rows_gather(own_kv)
        keys, values = both[:, :all_kv], both[:, all_kv:]
        mixed, log_norm = attend_forward(queries, keys, values, allowed)
        hidden = residual + contract(mixed, out_full, 1, 1)
        ffn_normed, ffn_scale = norm_forward(hidden, feedforward_gain[layer])
        ffn_all = rows_gather(ffn_normed)
        gate = contract(ffn_all, gate_full, 1, 1)
        up = contract(ffn_all, up_full, 1, 1)
        activated = (gate * jax.nn.sigmoid(gate) * up).astype(LOW)
        ffn_out = rows_scatter(contract(activated, down_full, 1, 0))
        saved.append(
            (residual, mixer_scale, normed, queries, keys, values, log_norm, mixed, hidden)
            + (ffn_scale, ffn_all, gate, up, activated)
        )
        residual = hidden + ffn_out

    weight_grads = [None] * layer_total
    gain_grads = [None] * layer_total
    grad = to_token_blocks(cotangent).astype(jnp.float32)
    for layer in reversed(range(layer_total)):
        joint_full, out_full = attention_ws[layer]
        gate_full, up_full, down_full = ffn_ws[layer]
        (layer_input, mixer_scale, normed, queries, keys, values, log_norm, mixed, hidden) = saved[
            layer
        ][:9]
        ffn_scale, ffn_all, gate, up, activated = saved[layer][9:]
        grad_all = rows_gather(grad.astype(LOW))
        grad_act = contract(grad_all, down_full, 1, 1)
        down_grad = contract(activated, grad_all, 0, 0)
        sig = jax.nn.sigmoid(gate)
        grad_gate = (grad_act * up * sig * (1.0 + gate * (1.0 - sig))).astype(LOW)
        grad_up = (grad_act * gate * sig).astype(LOW)
        grad_ffn_normed = rows_scatter(
            contract(grad_gate, gate_full, 1, 0) + contract(grad_up, up_full, 1, 0)
        )
        gate_grad = contract(grad_gate, ffn_all, 0, 0)
        up_grad = contract(grad_up, ffn_all, 0, 0)
        ffn_norm_grad, ffn_gain_grad = norm_backward(
            grad_ffn_normed, hidden, ffn_scale, feedforward_gain[layer]
        )
        grad_hidden = grad + ffn_norm_grad
        grad_low = grad_hidden.astype(LOW)
        grad_mixed = contract(grad_low, out_full, 1, 0).astype(LOW)
        out_grad = contract(grad_low, mixed, 0, 0)
        grad_query, grad_key, grad_value = attend_backward(
            queries, keys, values, log_norm, grad_mixed, allowed
        )
        grad_kv = rows_scatter(jnp.concatenate([grad_key, grad_value], 1))
        grad_joint = jnp.concatenate(
            [
                rotate(grad_query, cosine, -sine) * head_scale,
                rotate(grad_kv[:, :all_kv], cosine, -sine),
                grad_kv[:, all_kv:],
            ],
            1,
        ).astype(LOW)
        grad_normed = contract(grad_joint, joint_full, 1, 1)
        joint_grad = contract(normed, grad_joint, 0, 0)
        mixer_norm_grad, mixer_gain_grad = norm_backward(
            grad_normed, layer_input, mixer_scale, attention_gain[layer]
        )
        grad = grad_hidden + mixer_norm_grad
        ffn_parts = ffn_grads([gate_grad, up_grad, down_grad])
        weight_grads[layer] = attention_grads(joint_grad, out_grad) + (
            ffn_parts[0],
            ffn_parts[1],
            ffn_parts[2],
        )
        gain_grads[layer] = jnp.stack([mixer_gain_grad, ffn_gain_grad])

    gain_total = lax.psum(jnp.stack(gain_grads), ("dp", "rows", "cols"))
    totals = [jnp.stack([weight_grads[n][i] for n in range(layer_total)]) for i in range(7)]
    return (
        to_feature_blocks(residual),
        to_feature_blocks(grad),
        totals[0],
        totals[1],
        totals[2],
        totals[3],
        totals[4],
        totals[5],
        totals[6],
        gain_total[:, 0],
        gain_total[:, 1],
    )


def solution(mesh):
    whole = P("rows", ("dp", "cols"))
    weight = P(None, "rows", "cols")
    flipped = P(None, "cols", "rows")
    return jax.shard_map(
        on_device,
        mesh=mesh,
        in_specs=(whole, weight, weight, weight, flipped, weight, weight, weight)
        + (P(), P(), P("dp", None), P("dp", None), whole),
        out_specs=(whole, whole, weight, weight, weight, flipped, weight, weight, weight, P(), P()),
        check_vma=False,
    )
```

time: 2400 us -> 885 us (0.37)
  waiting for transfers between devices: 1720 us -> 297 us
  blocking collectives: 253 us -> 120 us
  local copies, waits for them, and re-layouts: 35 us -> 121 us
  other arithmetic: 113 us -> 71.1 us
    reduce_scatter x20 -> x14, waiting for transfers between devices: 1010 us -> 34.3 us  [the longest x2 34.2 us: attention_grads(): joint = dp_total(lax.psum_scatter(part, 'cols', scatter_dimension=0))]
    all_gather x16 -> x10, waiting for transfers between devices: 612 us -> 44 us  [the longest x6 43.9 us: ffn_weights(): lax.all_gather(whole[i], 'cols', axis=0, tiled=True)]
    ppermute x0 -> x54, waiting for transfers between devices: none -> 218 us  [the longest x48 172 us: swap_rows(): return lax.ppermute(value, 'rows', [(i, i ^ step) for i in range(count)])]
    all_to_all x4 -> x0, blocking collectives: 79.4 us -> none  [to_head_blocks(): lax.all_to_all(values, 'cols', split_axis=1, concat_axis=0, tiled=True)]
    psum x1 -> x0, waiting for transfers between devices: 66.9 us -> none  [on_device(): lax.psum(jnp.stack(query_grads).astype(jnp.bfloat16), 'dp')]
    psum x9 -> x1, blocking collectives: 90.8 us -> 40.5 us  [on_device(): gain_total = lax.psum(jnp.stack(gain_grads), ('dp', 'rows', 'cols'))]
    ppermute x0 -> x54, starting transfers between devices: none -> 36.7 us  [the longest x48 30.1 us: swap_rows(): return lax.ppermute(value, 'rows', [(i, i ^ step) for i in range(count)])]
    convert_element_type x36 -> x25, other arithmetic: 51.6 us -> 19.6 us  [the longest x10 8.27 us: one_group(): grad_scores = (probs * (grad_probs - inner)).astype(LOW)]
  transfers between devices with their start and end apart: 41 -> 78, of which waited for: 37 -> 33; matrix products, arithmetic and copies ran while one was open for 4% -> 42% of each run, Pallas kernels for 0% -> 0%
where the time goes in v1:
time: 885 us; the launch traced here: 875 us
  waiting for transfers between devices  297 us (34%)
  matrix products  208 us (24%)
  local copies, waits for them, and re-layouts  121 us (14%)
  blocking collectives  120 us (14%)
  other arithmetic  71.1 us (8%)
  starting transfers between devices  39.2 us (4%)
  between operations  17.8 us (2%)
    ppermute x48, waiting for transfers between devices, swap_rows(): return lax.ppermute(value, 'rows', [(i, i ^ step) for i in range(count)])  172 us
    dot_general x30, matrix products, contract(): lax.dot_general(left, right, (((left_dim,), (right_dim,)), ((), ())), pre...  102 us
    ppermute x6, waiting for transfers between devices, dp_total(): other = lax.ppermute(value, 'dp', [(0, 1), (1, 0)])  46 us
    all_gather x6, waiting for transfers between devices, ffn_weights(): lax.all_gather(whole[i], 'cols', axis=0, tiled=True)  43.9 us
    all_gather x2, blocking collectives, attention_weights(): wide = lax.all_gather(joint, 'cols', axis=0)  41.6 us
    psum x1, blocking collectives, on_device(): gain_total = lax.psum(jnp.stack(gain_grads), ('dp', 'rows', 'cols'))  40.5 us
    all_gather x2, blocking collectives, attention_weights(): out_wide = unspread(lax.all_gather(out_weight[layer].T, 'cols', axis=0))  37.7 us
    unnamed x302, local copies, waits for them, and re-layouts  36.4 us
  transfers between devices with their start and end apart: 78, of which 33 were waited for; matrix products, arithmetic and copies ran while one was open for 42% of the time, Pallas kernels for 0%

profile of v1, /device:TPU:0, one launch (start us, length us, event | category | flops | bytes accessed | tf_op | source)
XLA Modules:
  0.0 874.7 jit_solution(1743110791103319822)
XLA Ops:
  9.2 21.7 %all-gather.4 = bf16[4,240,400]{1,2,0:T(8,128)(2,1)S(1)} all-gather(bf16[1,240,400]{1,2,0:T(8,128)(2,1)S(1)} %maximum_bitcast_fusion), channel_id=2, replica_groups=mesh['dp'=2,'rows'=4,'cols'=4] {'cols'}, dimensions={0}, use_global_device_ids=true | all-gather | bytes 960000 | tf_op jit(solution)/shard_map/all_gather | solution.py:244
  33.3 15.7 %all-gather.1 = bf16[960,240]{1,0:T(8,128)(2,1)S(1)} all-gather(bf16[240,240]{1,0:T(8,128)(2,1)S(1)} %bitcast.712), channel_id=3, replica_groups=mesh['dp'=2,'rows'=4,'cols'=4] {'cols'}, dimensions={0}, use_global_device_ids=true | all-gather | bytes 576000 | tf_op jit(solution)/shard_map/all_gather | solution.py:254
  55.5 9.0 %collective-permute-done.8 = bf16[1,3,160,240]{3,2,0,1:T(8,128)(2,1)S(1)} collective-permute-done((bf16[1,3,160,240]{3,2,0,1:T(8,128)(2,1)S(1)}, bf16[1,3,160,240]{3,2,0,1:T(8,128)(2,1)S(1)}, u32[]{:S(2)}, u32[]{:S(2)}) %collective-permute-start.8) | collective-permute-done | bytes 230432 | tf_op jit(solution)/shard_map/ppermute | solution.py:40
  64.6 5.0 collective-permute-done.9
  77.6 19.9 %all-gather.5 = bf16[4,240,400]{1,2,0:T(8,128)(2,1)S(1)} all-gather(bf16[1,240,400]{1,2,0:T(8,128)(2,1)S(1)} %maximum_bitcast_fusion.1), channel_id=4, replica_groups=mesh['dp'=2,'rows'=4,'cols'=4] {'cols'}, dimensions={0}, use_global_device_ids=true | all-gather | bytes 960000 | tf_op jit(solution)/shard_map/all_gather | solution.py:244
  112.9 3.5 convolution_convert_fusion.3
  117.3 7.2 collective-permute-done.3
  129.1 19.0 %while.56 = (s32[]{:T(128)}, bf16[5,3,256,64]{2,3,1,0:T(8,128)(2,1)S(1)}, f32[5,3,256]{2,1,0:T(4,128)S(1)}, bf16[5,3,256,64]{2,3,1,0:T(8,128)(2,1)S(1)}, bf16[5,...) while((s32[]{:T(128)}, ...), condition=%wide.region_4.5_spmd.clone, body=%wide.region_1.4_spmd.clone.sunk | while | flops 209190144 | bytes 11084913 | solution.py:132
  153.2 11.7 %collective-permute-done.5 = bf16[256,960]{0,1:T(8,128)(2,1)} collective-permute-done((bf16[256,960]{0,1:T(8,128)(2,1)S(1)}, bf16[256,960]{0,1:T(8,128)(2,1)}, u32[]{:S(2)}, u32[]{:S(2)}) %collective-permute-start.5) | collective-permute-done | bytes 491552 | tf_op jit(solution)/shard_map/ppermute | solution.py:40
  169.9 22.0 %all-gather.3 = bf16[960,240]{1,0:T(8,128)(2,1)S(1)} all-gather(bf16[240,240]{1,0:T(8,128)(2,1)S(1)} %bitcast.713), channel_id=5, replica_groups=mesh['dp'=2,'rows'=4,'cols'=4] {'cols'}, dimensions={0}, use_global_device_ids=true | all-gather | bytes 576000 | tf_op jit(solution)/shard_map/all_gather | solution.py:254
  197.8 5.1 fusion.176
  202.9 6.1 multiply_convert_fusion.7
  209.0 5.5 fusion.209
  225.6 16.1 %collective-permute-done.11 = bf16[256,960]{0,1:T(8,128)(2,1)} collective-permute-done((bf16[256,960]{0,1:T(8,128)(2,1)}, bf16[256,960]{0,1:T(8,128)(2,1)}, u32[]{:S(2)}, u32[]{:S(2)}) %collective-permute-start.11) | collective-permute-done | bytes 491552 | tf_op jit(solution)/shard_map/ppermute | solution.py:40
  243.5 3.8 convolution_convert_fusion.2
  254.8 11.0 %collective-permute-done.12 = bf16[256,640]{0,1:T(8,128)(2,1)S(1)} collective-permute-done((bf16[256,640]{0,1:T(8,128)(2,1)}, bf16[256,640]{0,1:T(8,128)(2,1)S(1)}, u32[]{:S(2)}, u32[]{:S(2)}) %collective-permute-start.12) | collective-permute-done | bytes 327712 | tf_op jit(solution)/shard_map/ppermute | solution.py:40
  278.0 19.0 %while.57 = (s32[]{:T(128)}, bf16[5,3,256,64]{2,3,1,0:T(8,128)(2,1)S(1)}, f32[5,3,256]{2,1,0:T(4,128)S(1)}, bf16[5,3,256,64]{2,3,1,0:T(8,128)(2,1)S(1)}, bf16[5,...) while((s32[]{:T(128)}, ...), condition=%wide.region_10.11_spmd.clone, body=%wide.region_7.10_spmd.clone.sunk | while | flops 209190144 | bytes 11084913 | solution.py:132
  304.2 9.5 %collective-permute-done.14 = bf16[256,960]{0,1:T(8,128)(2,1)S(1)} collective-permute-done((bf16[256,960]{0,1:T(8,128)(2,1)S(1)}, bf16[256,960]{0,1:T(8,128)(2,1)S(1)}, u32[]{:S(2)}, u32[]{:S(2)}) %collective-permute-start.14) | collective-permute-done | bytes 491552 | tf_op jit(solution)/shard_map/ppermute | solution.py:40
  320.8 5.0 fusion.173
  325.8 15.8 %all-gather.31.cloned.1.call-done = bf16[640,960]{1,0:T(8,128)(2,1)} async-done(((bf16[160,960]{1,0:T(8,128)(2,1)}), bf16[640,960]{1,0:T(8,128)(2,1)}) %all-gather.31.cloned.1.call-update) | async-done | bytes 1228816 | tf_op jit(solution)/shard_map/all_gather | solution.py:264
  341.6 5.0 fusion.174
  346.6 28.1 %all-gather.35.cloned.1.call-done = bf16[640,960]{1,0:T(8,128)(2,1)} async-done(((bf16[160,960]{1,0:T(8,128)(2,1)}), bf16[640,960]{1,0:T(8,128)(2,1)}) %all-gather.35.cloned.1.call-update) | async-done | bytes 1228816 | tf_op jit(solution)/shard_map/all_gather | solution.py:264
  374.7 6.2 multiply_convert_fusion.4
  392.6 10.5 %collective-permute-done.30 = bf16[256,960]{0,1:T(8,128)(2,1)S(1)} collective-permute-done((bf16[256,960]{0,1:T(8,128)(2,1)S(1)}, bf16[256,960]{0,1:T(8,128)(2,1)S(1)}, u32[]{:S(2)}, u32[]{:S(2)}) %collective-permute-start.30) | collective-permute-done | bytes 491552 | tf_op jit(solution)/shard_map/ppermute | solution.py:40
  403.6 9.5 %collective-permute-done.20 = bf16[256,960]{0,1:T(8,128)(2,1)S(1)} collective-permute-done((bf16[256,960]{0,1:T(8,128)(2,1)S(1)}, bf16[256,960]{0,1:T(8,128)(2,1)S(1)}, u32[]{:S(2)}, u32[]{:S(2)}) %collective-permute-start.20) | collective-permute-done | bytes 491552 | tf_op jit(solution)/shard_map/ppermute | solution.py:40
  418.5 4.4 convolution_convert_fusion.8
  423.0 4.4 convolution_convert_fusion.6
  432.1 45.6 %while.58 = (s32[]{:T(128)}, f32[5,3,256,64]{2,3,1,0:T(8,128)}, f32[5,1024,64]{1,2,0:T(8,128)S(1)}, f32[5,1024,64]{1,2,0:T(8,128)S(1)}, bf16[5,3,256,64]{2,3,1,0...) while((s32[]{:T(128)}, f32[5,3,256,64]{2,3,1,0:T(8,128)}, ...), condition=%wide.region_15.16_spmd.clone, body=%wide.region_13.15_spmd.clone.sunk | while | flops 513539328 | bytes 26186888 | solution.py:161
  485.3 7.4 collective-permute-done.32
  497.0 10.4 %collective-permute-done.33 = bf16[256,960]{0,1:T(8,128)(2,1)S(1)} collective-permute-done((bf16[256,960]{0,1:T(8,128)(2,1)S(1)}, bf16[256,960]{0,1:T(8,128)(2,1)S(1)}, u32[]{:S(2)}, u32[]{:S(2)}) %collective-permute-start.33) | collective-permute-done | bytes 491552 | tf_op jit(solution)/shard_map/ppermute | solution.py:40
  516.6 7.0 multiply_convert_fusion.2
  523.6 3.7 convolution_convert_fusion.10
  527.4 3.6 fusion.214
  531.0 3.7 fusion.212
  536.6 3.8 convolution_convert_fusion.11
  543.8 11.8 %collective-permute-done.36 = bf16[256,960]{0,1:T(8,128)(2,1)S(1)} collective-permute-done((bf16[256,960]{0,1:T(8,128)(2,1)S(1)}, bf16[256,960]{0,1:T(8,128)(2,1)S(1)}, u32[]{:S(2)}, u32[]{:S(2)}) %collective-permute-start.36) | collective-permute-done | bytes 491552 | tf_op jit(solution)/shard_map/ppermute | solution.py:40
  564.0 4.4 collective-permute-done.22
  578.2 49.0 %while.59 = (s32[]{:T(128)}, f32[5,3,256,64]{2,3,1,0:T(8,128)}, f32[5,1024,64]{1,2,0:T(8,128)S(1)}, f32[5,1024,64]{1,2,0:T(8,128)S(1)}, bf16[5,3,256,64]{2,3,1,0...) while((s32[]{:T(128)}, f32[5,3,256,64]{2,3,1,0:T(8,128)}, ...), condition=%wide.region_20.21_spmd.clone, body=%wide.region_18.20_spmd.clone.sunk | while | flops 513539328 | bytes 26187912 | solution.py:161
  638.9 8.1 collective-permute-done.38
  655.9 6.3 collective-permute-done.51
  669.2 20.6 %collective-permute-done.53 = bf16[3,240,640]{2,1,0:T(8,128)(2,1)S(1)} collective-permute-done((bf16[3,240,640]{2,1,0:T(8,128)(2,1)}, bf16[3,240,640]{2,1,0:T(8,128)(2,1)S(1)}, u32[]{:S(2)}, u32[]{:S(2)}) %collective-permute-start.53) | collective-permute-done | bytes 921632 | tf_op jit(solution)/shard_map/ppermute | solution.py:86
  704.9 40.5 %psum.7 = f32[2,2,960]{2,0,1:T(2,128)S(1)} all-reduce(f32[2,2,960]{2,0,1:T(2,128)S(1)} %pad_maximum_fusion.49), channel_id=1, replica_groups=mesh['dp'=2,'rows'=4,'cols'=4] {'dp','rows','cols'}, use_global_device_ids=true, to_apply=%region_40.41 | all-reduce | flops 3840 | bytes 30720 | tf_op jit(solution)/shard_map/psum | solution.py:386
  752.8 20.9 %collective-permute-done.41 = bf16[1,240,256]{2,1,0:T(8,128)(2,1)S(1)} collective-permute-done((bf16[1,240,256]{2,1,0:T(8,128)(2,1)S(1)}, bf16[1,240,256]{2,1,0:T(8,128)(2,1)S(1)}, u32[]{:S(2)}, u32[]{:S(2)}) %collective-permute-start.41) | collective-permute-done | bytes 122912 | tf_op jit(solution)/shard_map/ppermute | solution.py:40
  787.9 13.9 %collective-permute-done.49 = bf16[3,240,640]{2,1,0:T(8,128)(2,1)S(1)} collective-permute-done((bf16[3,240,640]{2,1,0:T(8,128)(2,1)}, bf16[3,240,640]{2,1,0:T(8,128)(2,1)S(1)}, u32[]{:S(2)}, u32[]{:S(2)}) %collective-permute-start.49) | collective-permute-done | bytes 921632 | tf_op jit(solution)/shard_map/ppermute | solution.py:86
  816.0 16.4 %reduce-scatter.21.cloned.1.call-done = bf16[1,240,400]{1,2,0:T(8,128)(2,1)} async-done(((bf16[4,240,400]{1,2,0:T(8,128)(2,1)}), bf16[1,240,400]{1,2,0:T(8,128)(2,1)}) %reduce-scatter.21.cloned.1.call-update) | async-done | bytes 192016 | tf_op jit(solution)/shard_map/reduce_scatter | solution.py:276
  834.7 4.1 collective-permute-done.43
  839.8 17.8 %reduce-scatter.17.cloned.1.call-done = bf16[1,240,400]{1,2,0:T(8,128)(2,1)} async-done(((bf16[4,240,400]{1,2,0:T(8,128)(2,1)}), bf16[1,240,400]{1,2,0:T(8,128)(2,1)}) %reduce-scatter.17.cloned.1.call-update) | async-done | bytes 192016 | tf_op jit(solution)/shard_map/reduce_scatter | solution.py:276
  859.1 4.9 collective-permute-done.42
  (863 shorter events, 385.3 us)
Async XLA Ops:
  7.2 105.7 %all-gather.17.cloned.1.call-start = ((), (), s32[]{:S(2)}) async-start(), calls=%async_computation.14 | async-start | bytes 3993600 | tf_op jit(solution)/shard_map/all_gather | solution.py:253
  32.5 115.7 %all-gather.19.cloned.1.call-start = ((), (), s32[]{:S(2)}) async-start(), calls=%async_computation.15 | async-start | bytes 2457600 | tf_op jit(solution)/shard_map/all_gather | solution.py:255
  50.2 147.6 %all-gather.21.cloned.1.call-start = ((), (), s32[]{:S(2)}) async-start(), calls=%async_computation.16 | async-start | bytes 1638400 | tf_op jit(solution)/shard_map/all_gather | solution.py:264
  55.1 14.5 %collective-permute-start.9 = (bf16[1,3,160,240]{3,2,0,1:T(8,128)(2,1)S(1)}, bf16[1,3,160,240]{3,2,0,1:T(8,128)(2,1)S(1)}, u32[]{:S(2)}, u32[]{:S(2)}) collective-permute-start(bf16[1,3,160,240]{3,2,0,1:T(8,128)(2,1)S(1)} %get-tuple-element.539), channel_id=1, source_target_pairs={{0,12},{4,8},{8,4},{12,0},{1,13},{5,9},{9,5},{13,1},{2,14},{6,10},... | collective-permute-start | bytes 691208 | tf_op jit(solution)/shard_map/ppermute | solution.py:40
  71.0 132.0 %all-gather.23.cloned.1.call-start = ((), (), s32[]{:S(2)}) async-start(), calls=%async_computation.17 | async-start | bytes 1638400 | tf_op jit(solution)/shard_map/all_gather | solution.py:264
  72.3 136.7 %all-gather.25.cloned.1.call-start = ((), (), s32[]{:S(2)}) async-start(), calls=%async_computation.18 | async-start | bytes 1638400 | tf_op jit(solution)/shard_map/all_gather | solution.py:264
  73.8 169.7 %all-gather.27.cloned.1.call-start = ((), (), s32[]{:S(2)}) async-start(), calls=%async_computation.19 | async-start | bytes 3993600 | tf_op jit(solution)/shard_map/all_gather | solution.py:253
  75.3 37.2 %collective-permute-start = (bf16[1,240,256]{2,1,0:T(8,128)(2,1)S(1)}, bf16[1,240,256]{2,1,0:T(8,128)(2,1)S(1)}, u32[]{:S(2)}, u32[]{:S(2)}) collective-permute-start(bf16[1,240,256]{2,1,0:T(8,128)(2,1)S(1)} %bitcast.728), channel_id=1, source_target_pairs={{0,4},{4,0},{8,12},{12,8},{1,5},{5,1},{9,13},{13,9},{2,6},{6,2},{1... | collective-permute-start | bytes 368648 | tf_op jit(solution)/shard_map/ppermute | solution.py:40
  75.5 37.0 %collective-permute-start.1 = (bf16[1,240,256]{2,1,0:T(8,128)(2,1)S(1)}, bf16[1,240,256]{2,1,0:T(8,128)(2,1)S(1)}, u32[]{:S(2)}, u32[]{:S(2)}) collective-permute-start(bf16[1,240,256]{2,1,0:T(8,128)(2,1)S(1)} %bitcast.727), channel_id=1, source_target_pairs={{0,8},{4,12},{8,0},{12,4},{1,9},{5,13},{9,1},{13,5},{2,10},{6,14},... | collective-permute-start | bytes 368648 | tf_op jit(solution)/shard_map/ppermute | solution.py:40
  76.0 36.6 %collective-permute-start.2 = (bf16[1,240,256]{2,1,0:T(8,128)(2,1)S(1)}, bf16[1,240,256]{2,1,0:T(8,128)(2,1)S(1)}, u32[]{:S(2)}, u32[]{:S(2)}) collective-permute-start(bf16[1,240,256]{2,1,0:T(8,128)(2,1)S(1)} %bitcast.726), channel_id=1, source_target_pairs={{0,12},{4,8},{8,4},{12,0},{1,13},{5,9},{9,5},{13,1},{2,14},{6,10},... | collective-permute-start | bytes 368648 | tf_op jit(solution)/shard_map/ppermute | solution.py:40
  99.1 198.0 %all-gather.29.cloned.1.call-start = ((), (), s32[]{:S(2)}) async-start(), calls=%async_computation.20 | async-start | bytes 2457600 | tf_op jit(solution)/shard_map/all_gather | solution.py:255
  167.0 29.3 %collective-permute-start.6 = (bf16[512,960]{0,1:T(8,128)(2,1)}, bf16[512,960]{0,1:T(8,128)(2,1)}, u32[]{:S(2)}, u32[]{:S(2)}) collective-permute-start(bf16[512,960]{0,1:T(8,128)(2,1)} %pad_maximum_fusion.11), channel_id=1, source_target_pairs={{0,4},{4,0},{8,12},{12,8},{1,5},{5,1},{9,13},{13,9},{2,6},{6,2},{1... | collective-permute-start | bytes 2949128 | tf_op jit(solution)/shard_map/ppermute | solution.py:40
  168.0 49.6 %collective-permute-start.16 = (bf16[1,3,160,240]{3,2,0,1:T(8,128)(2,1)}, bf16[1,3,160,240]{3,2,0,1:T(8,128)(2,1)}, u32[]{:S(2)}, u32[]{:S(2)}) collective-permute-start(bf16[1,3,160,240]{3,2,0,1:T(8,128)(2,1)} %get-tuple-element.531), channel_id=1, source_target_pairs={{0,4},{4,0},{8,12},{12,8},{1,5},{5,1},{9,13},{13,9},{2,6},{6,2},{1... | collective-permute-start | bytes 691208 | tf_op jit(solution)/shard_map/ppermute | solution.py:40
  168.5 52.9 %collective-permute-start.17 = (bf16[1,3,160,240]{3,2,0,1:T(8,128)(2,1)}, bf16[1,3,160,240]{3,2,0,1:T(8,128)(2,1)}, u32[]{:S(2)}, u32[]{:S(2)}) collective-permute-start(bf16[1,3,160,240]{3,2,0,1:T(8,128)(2,1)} %get-tuple-element.530), channel_id=1, source_target_pairs={{0,8},{4,12},{8,0},{12,4},{1,9},{5,13},{9,1},{13,5},{2,10},{6,14},... | collective-permute-start | bytes 691208 | tf_op jit(solution)/shard_map/ppermute | solution.py:40
  169.1 53.3 %collective-permute-start.18 = (bf16[1,3,160,240]{3,2,0,1:T(8,128)(2,1)}, bf16[1,3,160,240]{3,2,0,1:T(8,128)(2,1)}, u32[]{:S(2)}, u32[]{:S(2)}) collective-permute-start(bf16[1,3,160,240]{3,2,0,1:T(8,128)(2,1)} %get-tuple-element.529), channel_id=1, source_target_pairs={{0,12},{4,8},{8,4},{12,0},{1,13},{5,9},{9,5},{13,1},{2,14},{6,10},... | collective-permute-start | bytes 691208 | tf_op jit(solution)/shard_map/ppermute | solution.py:40
  193.2 127.6 %all-gather.33.cloned.1.call-start = ((), (), s32[]{:S(2)}) async-start(), calls=%async_computation.22 | async-start | bytes 1638400 | tf_op jit(solution)/shard_map/all_gather | solution.py:264
  220.9 20.8 %collective-permute-start.11 = (bf16[256,960]{0,1:T(8,128)(2,1)}, bf16[256,960]{0,1:T(8,128)(2,1)}, u32[]{:S(2)}, u32[]{:S(2)}) collective-permute-start(bf16[256,960]{0,1:T(8,128)(2,1)} %fusion.114), channel_id=1, source_target_pairs={{0,8},{4,12},{8,0},{12,4},{1,9},{5,13},{9,1},{13,5},{2,10},{6,14},... | collective-permute-start | bytes 1474568 | tf_op jit(solution)/shard_map/ppermute | solution.py:40
  225.5 116.1 %all-gather.31.cloned.1.call-start = ((), (), s32[]{:S(2)}) async-start(), calls=%async_computation.21 | async-start | bytes 1638400 | tf_op jit(solution)/shard_map/all_gather | solution.py:264
  248.2 17.6 %collective-permute-start.12 = (bf16[256,640]{0,1:T(8,128)(2,1)}, bf16[256,640]{0,1:T(8,128)(2,1)S(1)}, u32[]{:S(2)}, u32[]{:S(2)}) collective-permute-start(bf16[256,640]{0,1:T(8,128)(2,1)} %pad_maximum_fusion.42), channel_id=1, source_target_pairs={{0,8},{4,12},{8,0},{12,4},{1,9},{5,13},{9,1},{13,5},{2,10},{6,14},... | collective-permute-start | bytes 983048 | tf_op jit(solution)/shard_map/ppermute | solution.py:40
  250.2 16.4 %collective-permute-start.24 = (bf16[1,240,256]{2,1,0:T(8,128)(2,1)S(1)}, bf16[1,240,256]{2,1,0:T(8,128)(2,1)}, u32[]{:S(2)}, u32[]{:S(2)}) collective-permute-start(bf16[1,240,256]{2,1,0:T(8,128)(2,1)S(1)} %bitcast.731), channel_id=1, source_target_pairs={{0,4},{4,0},{8,12},{12,8},{1,5},{5,1},{9,13},{13,9},{2,6},{6,2},{1... | collective-permute-start | bytes 368648 | tf_op jit(solution)/shard_map/ppermute | solution.py:40
  250.3 20.7 %collective-permute-start.25 = (bf16[1,240,256]{2,1,0:T(8,128)(2,1)S(1)}, bf16[1,240,256]{2,1,0:T(8,128)(2,1)S(1)}, u32[]{:S(2)}, u32[]{:S(2)}) collective-permute-start(bf16[1,240,256]{2,1,0:T(8,128)(2,1)S(1)} %bitcast.730), channel_id=1, source_target_pairs={{0,8},{4,12},{8,0},{12,4},{1,9},{5,13},{9,1},{13,5},{2,10},{6,14},... | collective-permute-start | bytes 368648 | tf_op jit(solution)/shard_map/ppermute | solution.py:40
  252.1 20.7 %collective-permute-start.26 = (bf16[1,240,256]{2,1,0:T(8,128)(2,1)S(1)}, bf16[1,240,256]{2,1,0:T(8,128)(2,1)S(1)}, u32[]{:S(2)}, u32[]{:S(2)}) collective-permute-start(bf16[1,240,256]{2,1,0:T(8,128)(2,1)S(1)} %bitcast.729), channel_id=1, source_target_pairs={{0,12},{4,8},{8,4},{12,0},{1,13},{5,9},{9,5},{13,1},{2,14},{6,10},... | collective-permute-start | bytes 368648 | tf_op jit(solution)/shard_map/ppermute | solution.py:40
  273.4 28.4 %collective-permute-start.27 = (bf16[256,960]{0,1:T(8,128)(2,1)}, bf16[256,960]{0,1:T(8,128)(2,1)}, u32[]{:S(2)}, u32[]{:S(2)}) collective-permute-start(bf16[256,960]{0,1:T(8,128)(2,1)} %bitcast.105), channel_id=1, source_target_pairs={{0,8},{4,12},{8,0},{12,4},{1,9},{5,13},{9,1},{13,5},{2,10},{6,14},... | collective-permute-start | bytes 1474568 | tf_op jit(solution)/shard_map/ppermute | solution.py:40
  275.2 99.5 %all-gather.35.cloned.1.call-start = ((), (), s32[]{:S(2)}) async-start(), calls=%async_computation.23 | async-start | bytes 1638400 | tf_op jit(solution)/shard_map/all_gather | solution.py:264
  316.1 192.4 %reduce-scatter.27.cloned.1.call-start = ((), (), s32[]{:S(2)}) async-start(), calls=%async_computation.30 | async-start | bytes 2457600 | tf_op jit(solution)/shard_map/reduce_scatter | solution.py:277
  391.1 22.0 %collective-permute-start.20 = (bf16[256,960]{0,1:T(8,128)(2,1)S(1)}, bf16[256,960]{0,1:T(8,128)(2,1)S(1)}, u32[]{:S(2)}, u32[]{:S(2)}) collective-permute-start(bf16[256,960]{0,1:T(8,128)(2,1)S(1)} %fusion.110), channel_id=1, source_target_pairs={{0,8},{4,12},{8,0},{12,4},{1,9},{5,13},{9,1},{13,5},{2,10},{6,14},... | collective-permute-start | bytes 1474568 | tf_op jit(solution)/shard_map/ppermute | solution.py:40
  417.5 156.2 %reduce-scatter.37.cloned.1.call-start = ((), (), s32[]{:S(2)}) async-start(), calls=%async_computation.35 | async-start | bytes 1638400 | tf_op jit(solution)/shard_map/reduce_scatter | solution.py:289
  422.9 206.6 %reduce-scatter.41.cloned.1.call-start = ((), (), s32[]{:S(2)}) async-start(), calls=%async_computation.37 | async-start | bytes 1638400 | tf_op jit(solution)/shard_map/reduce_scatter | solution.py:289
  427.4 203.4 %reduce-scatter.39.cloned.1.call-start = ((), (), s32[]{:S(2)}) async-start(), calls=%async_computation.36 | async-start | bytes 1638400 | tf_op jit(solution)/shard_map/reduce_scatter | solution.py:289
  482.3 210.5 %reduce-scatter.29.cloned.1.call-start = ((), (), s32[]{:S(2)}) async-start(), calls=%async_computation.31 | async-start | bytes 614400 | tf_op jit(solution)/shard_map/reduce_scatter | solution.py:278
  510.6 190.3 %reduce-scatter.35.cloned.1.call-start = ((), (), s32[]{:S(2)}) async-start(), calls=%async_computation.34 | async-start | bytes 1638400 | tf_op jit(solution)/shard_map/reduce_scatter | solution.py:289
  516.3 185.9 %reduce-scatter.33.cloned.1.call-start = ((), (), s32[]{:S(2)}) async-start(), calls=%async_computation.33 | async-start | bytes 1638400 | tf_op jit(solution)/shard_map/reduce_scatter | solution.py:289
  527.3 176.3 %reduce-scatter.31.cloned.1.call-start = ((), (), s32[]{:S(2)}) async-start(), calls=%async_computation.32 | async-start | bytes 1638400 | tf_op jit(solution)/shard_map/reduce_scatter | solution.py:289
  540.4 235.3 %reduce-scatter.23.cloned.1.call-start = ((), (), s32[]{:S(2)}) async-start(), calls=%async_computation.28 | async-start | bytes 2457600 | tf_op jit(solution)/shard_map/reduce_scatter | solution.py:277
  561.0 218.3 %reduce-scatter.19.cloned.1.call-start = ((), (), s32[]{:S(2)}) async-start(), calls=%async_computation.26 | async-start | bytes 3993600 | tf_op jit(solution)/shard_map/reduce_scatter | solution.py:267
  573.7 231.0 %reduce-scatter.15.cloned.1.call-start = ((), (), s32[]{:S(2)}) async-start(), calls=%async_computation.24 | async-start | bytes 3993600 | tf_op jit(solution)/shard_map/reduce_scatter | solution.py:267
  635.7 19.2 %collective-permute-start.50 = (bf16[1,3,160,240]{3,2,1,0:T(8,128)(2,1)}, bf16[1,3,160,240]{3,2,1,0:T(8,128)(2,1)}, u32[]{:S(2)}, u32[]{:S(2)}) collective-permute-start(bf16[1,3,160,240]{3,2,1,0:T(8,128)(2,1)} %get-tuple-element.517), channel_id=1, source_target_pairs={{0,4},{4,0},{8,12},{12,8},{1,5},{5,1},{9,13},{13,9},{2,6},{6,2},{1... | collective-permute-start | bytes 691208 | tf_op jit(solution)/shard_map/ppermute | solution.py:40
  651.9 162.0 %reduce-scatter.25.cloned.1.call-start = ((), (), s32[]{:S(2)}) async-start(), calls=%async_computation.29 | async-start | bytes 614400 | tf_op jit(solution)/shard_map/reduce_scatter | solution.py:278
  666.5 23.3 %collective-permute-start.53 = (bf16[3,240,640]{2,1,0:T(8,128)(2,1)}, bf16[3,240,640]{2,1,0:T(8,128)(2,1)S(1)}, u32[]{:S(2)}, u32[]{:S(2)}) collective-permute-start(bf16[3,240,640]{2,1,0:T(8,128)(2,1)} %copy.175), channel_id=1, source_target_pairs={{0,16},{16,0},{1,17},{17,1},{2,18},{18,2},{3,19},{19,3},{4,20},{20... | collective-permute-start | bytes 2764808 | tf_op jit(solution)/shard_map/ppermute | solution.py:86
  700.8 49.5 %collective-permute-start.39 = (bf16[1,240,256]{2,1,0:T(8,128)(2,1)S(1)}, bf16[1,240,256]{2,1,0:T(8,128)(2,1)S(1)}, u32[]{:S(2)}, u32[]{:S(2)}) collective-permute-start(bf16[1,240,256]{2,1,0:T(8,128)(2,1)S(1)} %get-tuple-element.562), channel_id=1, source_target_pairs={{0,4},{4,0},{8,12},{12,8},{1,5},{5,1},{9,13},{13,9},{2,6},{6,2},{1... | collective-permute-start | bytes 368648 | tf_op jit(solution)/shard_map/ppermute | solution.py:40
  746.2 31.6 %collective-permute-start.46 = (bf16[1,3,160,240]{3,2,1,0:T(8,128)(2,1)S(1)}, bf16[1,3,160,240]{3,2,1,0:T(8,128)(2,1)S(1)}, u32[]{:S(2)}, u32[]{:S(2)}) collective-permute-start(bf16[1,3,160,240]{3,2,1,0:T(8,128)(2,1)S(1)} %get-tuple-element.514), channel_id=1, source_target_pairs={{0,4},{4,0},{8,12},{12,8},{1,5},{5,1},{9,13},{13,9},{2,6},{6,2},{1... | collective-permute-start | bytes 691208 | tf_op jit(solution)/shard_map/ppermute | solution.py:40
  748.8 29.1 %collective-permute-start.47 = (bf16[1,3,160,240]{3,2,1,0:T(8,128)(2,1)S(1)}, bf16[1,3,160,240]{3,2,1,0:T(8,128)(2,1)S(1)}, u32[]{:S(2)}, u32[]{:S(2)}) collective-permute-start(bf16[1,3,160,240]{3,2,1,0:T(8,128)(2,1)S(1)} %get-tuple-element.513), channel_id=1, source_target_pairs={{0,8},{4,12},{8,0},{12,4},{1,9},{5,13},{9,1},{13,5},{2,10},{6,14},... | collective-permute-start | bytes 691208 | tf_op jit(solution)/shard_map/ppermute | solution.py:40
  748.8 29.1 %collective-permute-start.48 = (bf16[1,3,160,240]{3,2,1,0:T(8,128)(2,1)S(1)}, bf16[1,3,160,240]{3,2,1,0:T(8,128)(2,1)S(1)}, u32[]{:S(2)}, u32[]{:S(2)}) collective-permute-start(bf16[1,3,160,240]{3,2,1,0:T(8,128)(2,1)S(1)} %get-tuple-element.512), channel_id=1, source_target_pairs={{0,12},{4,8},{8,4},{12,0},{1,13},{5,9},{9,5},{13,1},{2,14},{6,10},... | collective-permute-start | bytes 691208 | tf_op jit(solution)/shard_map/ppermute | solution.py:40
  750.3 23.4 %collective-permute-start.41 = (bf16[1,240,256]{2,1,0:T(8,128)(2,1)S(1)}, bf16[1,240,256]{2,1,0:T(8,128)(2,1)S(1)}, u32[]{:S(2)}, u32[]{:S(2)}) collective-permute-start(bf16[1,240,256]{2,1,0:T(8,128)(2,1)S(1)} %get-tuple-element.560), channel_id=1, source_target_pairs={{0,12},{4,8},{8,4},{12,0},{1,13},{5,9},{9,5},{13,1},{2,14},{6,10},... | collective-permute-start | bytes 368648 | tf_op jit(solution)/shard_map/ppermute | solution.py:40
  777.8 54.5 %reduce-scatter.21.cloned.1.call-start = ((), (), s32[]{:S(2)}) async-start(), calls=%async_computation.27 | async-start | bytes 1024000 | tf_op jit(solution)/shard_map/reduce_scatter | solution.py:276
  779.4 22.4 %collective-permute-start.49 = (bf16[3,240,640]{2,1,0:T(8,128)(2,1)}, bf16[3,240,640]{2,1,0:T(8,128)(2,1)S(1)}, u32[]{:S(2)}, u32[]{:S(2)}) collective-permute-start(bf16[3,240,640]{2,1,0:T(8,128)(2,1)} %copy.166), channel_id=1, source_target_pairs={{0,16},{16,0},{1,17},{17,1},{2,18},{18,2},{3,19},{19,3},{4,20},{20... | collective-permute-start | bytes 2764808 | tf_op jit(solution)/shard_map/ppermute | solution.py:86
  783.2 74.4 %reduce-scatter.17.cloned.1.call-start = ((), (), s32[]{:S(2)}) async-start(), calls=%async_computation.25 | async-start | bytes 1024000 | tf_op jit(solution)/shard_map/reduce_scatter | solution.py:276
  813.9 19.9 %collective-permute-start.44 = (bf16[240,240]{0,1:T(8,128)(2,1)}, bf16[240,240]{0,1:T(8,128)(2,1)S(1)}, u32[]{:S(2)}, u32[]{:S(2)}) collective-permute-start(bf16[240,240]{0,1:T(8,128)(2,1)} %bitcast.733), channel_id=1, source_target_pairs={{0,16},{16,0},{1,17},{17,1},{2,18},{18,2},{3,19},{19,3},{4,20},{20... | collective-permute-start | bytes 345608 | tf_op jit(solution)/shard_map/ppermute | solution.py:86
  (147 other events, 1118.5 us)
Sparse Core Ops, SparseCore 0:
  32.6 30.7 all-gather.16
  65.5 28.9 all-gather.18
  96.1 32.4 all-gather.20
  130.0 31.6 all-gather.22
  163.1 39.5 all-gather.24
  204.7 35.1 all-gather.26
  241.4 32.8 all-gather.28
  275.8 32.5 all-gather.32
  309.9 31.6 all-gather.30
  343.0 31.6 all-gather.34
  417.6 29.4 reduce-scatter.26
  449.3 31.3 reduce-scatter.36
  483.0 30.0 reduce-scatter.40
  515.2 30.0 reduce-scatter.38
  547.5 20.1 reduce-scatter.28
  569.8 29.7 reduce-scatter.34
  601.8 30.0 reduce-scatter.32
  634.0 30.1 reduce-scatter.30
  666.7 29.0 reduce-scatter.22
  698.2 38.4 reduce-scatter.18
  739.2 44.9 reduce-scatter.14
  787.1 20.8 reduce-scatter.24
  810.3 22.0 reduce-scatter.20
  834.5 23.0 reduce-scatter.16

commit v2 on v1

v2 whole, which is shorter than its diff:
```python
import jax
import jax.numpy as jnp
from jax import lax
from jax.experimental import pallas as pl
from jax.sharding import PartitionSpec as P

HEADS = 15
KV_HEADS = 5
HEAD = 64
SEQ = 1024
GROUPS = HEADS // KV_HEADS
EPSILON = 1e-05
NEG_FILL = -1e30
ROPE_BASE = 100000.0
LOW = jnp.bfloat16


def contract(left, right, left_dim, right_dim):
    return lax.dot_general(
        left, right, (((left_dim,), (right_dim,)), ((), ())), preferred_element_type=jnp.float32
    )


def rope_tables(positions):
    half_dim = HEAD // 2
    frequency = ROPE_BASE ** (-2.0 * jnp.arange(half_dim, dtype=jnp.float32) / HEAD)
    angle = frequency[:, None] * positions.astype(jnp.float32)[None, :]
    return jnp.cos(angle), jnp.sin(angle)


def swap_rows(value, step):
    count = lax.axis_size("rows")
    return lax.ppermute(value, "rows", [(i, i ^ step) for i in range(count)])


def rows_gather(block):
    count = lax.axis_size("rows")
    blocks = {0: block}
    step = count // 2
    while step:
        held = sorted(blocks)
        got = swap_rows(jnp.concatenate([blocks[i] for i in held], 0), step)
        for n, i in enumerate(held):
            blocks[i ^ step] = got[n * block.shape[0] : (n + 1) * block.shape[0]]
        step //= 2
    return jnp.concatenate([blocks[i] for i in range(count)], 0)


def rows_scatter(partial):
    count = lax.axis_size("rows")
    size = partial.shape[0] // count
    blocks = {i: partial[i * size : (i + 1) * size] for i in range(count)}
    step = 1
    while step < count:
        kept = [i for i in sorted(blocks) if not i & step]
        sent = jnp.concatenate([blocks[i ^ step] for i in kept], 0).astype(LOW)
        got = swap_rows(sent, step)
        blocks = {
            i: blocks[i] + got[n * size : (n + 1) * size].astype(jnp.float32)
            for n, i in enumerate(kept)
        }
        step *= 2
    return blocks[0]


def rows_exchange(chunks, row_index):
    count = lax.axis_size("rows")
    own = lax.dynamic_index_in_dim(chunks, row_index, 0)
    result = lax.dynamic_update_slice_in_dim(jnp.zeros_like(chunks), own, row_index, 0)
    for step in range(1, count):
        peer = row_index ^ step
        got = swap_rows(lax.dynamic_index_in_dim(chunks, peer, 0), step)
        result = lax.dynamic_update_slice_in_dim(result, got, peer, 0)
    return result


def swap_dp(value, step):
    count = lax.axis_size("dp")
    return lax.ppermute(value, "dp", [(i, i ^ step) for i in range(count)])


def spread(value, parts):
    return value.reshape(value.shape[0], parts, -1).transpose(1, 0, 2)


def unspread(value):
    return value.transpose(1, 0, 2).reshape(value.shape[1], -1)


def norm_forward(residual, gain):
    inv_rms = lax.rsqrt(jnp.mean(residual * residual, 1, keepdims=True) + EPSILON)
    return (residual * inv_rms * gain[None, :]).astype(LOW), inv_rms


def norm_backward(grad_normed, residual, inv_rms, gain):
    weighted = grad_normed * gain[None, :]
    summed = jnp.mean(weighted * residual, 1, keepdims=True)
    grad_residual = weighted * inv_rms - residual * (inv_rms**3 * summed)
    return grad_residual, jnp.sum(grad_normed * residual * inv_rms, 0)


def turn(values, cosine, sine):
    width, count = values.shape
    split = values.reshape(width // HEAD, 2, HEAD // 2, count)
    lower, upper = split[:, 0], split[:, 1]
    turned = jnp.stack([lower * cosine - upper * sine, upper * cosine + lower * sine], 1)
    return turned.reshape(width, count)


def forward_kernel(query_ref, key_ref, value_ref, bias_ref, mixed_ref, log_ref):
    parts, _, size = key_ref.shape
    for i in range(GROUPS):
        rows = pl.ds(i * HEAD, HEAD)
        query = query_ref[rows, :]
        scores = [
            contract(key_ref[j], query, 0, 0) + bias_ref[pl.ds(j * size, size), :]
            for j in range(parts)
        ]
        peak = jnp.max(scores[0], 0, keepdims=True)
        for j in range(1, parts):
            peak = jnp.maximum(peak, jnp.max(scores[j], 0, keepdims=True))
        total = jnp.zeros_like(peak)
        mixed = jnp.zeros((HEAD, query.shape[1]), jnp.float32)
        for j in range(parts):
            weights = jnp.exp(scores[j] - peak)
            total = total + jnp.sum(weights, 0, keepdims=True)
            mixed = mixed + contract(value_ref[j], weights.astype(LOW), 1, 0)
        mixed_ref[rows, :] = (mixed / total).astype(LOW)
        log_ref[0, pl.ds(i, 1), :] = peak + jnp.log(total)


def backward_kernel(
    query_ref, key_ref, value_ref, bias_ref, mixed_ref, log_ref, grad_ref,
    grad_query_ref, grad_key_ref, grad_value_ref,
):
    parts, _, size = key_ref.shape
    for i in range(GROUPS):
        rows = pl.ds(i * HEAD, HEAD)
        query, grad = query_ref[rows, :], grad_ref[rows, :]
        wide = grad.astype(jnp.float32)
        inner = jnp.sum(wide * mixed_ref[rows, :].astype(jnp.float32), 0, keepdims=True)
        log_norm = log_ref[0, pl.ds(i, 1), :]
        grad_query = jnp.zeros((HEAD, query.shape[1]), jnp.float32)
        for j in range(parts):
            key, value = key_ref[j], value_ref[j]
            scores = contract(key, query, 0, 0) + bias_ref[pl.ds(j * size, size), :]
            probs = jnp.exp(scores - log_norm)
            grad_probs = contract(value, grad, 0, 0)
            grad_scores = (probs * (grad_probs - inner)).astype(LOW)
            grad_query = grad_query + contract(key, grad_scores, 1, 0)
            grad_key = contract(query, grad_scores, 1, 1)
            grad_value = contract(grad, probs.astype(LOW), 1, 1)
            if i == 0:
                grad_key_ref[j] = grad_key
                grad_value_ref[j] = grad_value
            else:
                grad_key_ref[j] += grad_key
                grad_value_ref[j] += grad_value
        grad_query_ref[rows, :] = grad_query


def attention_specs(queries, both):
    parts, _, size = both.shape
    count = queries.shape[1]
    per_query = pl.BlockSpec((GROUPS * HEAD, count), lambda g: (g, 0))
    key = pl.BlockSpec((parts, HEAD, size), lambda g: (0, g, 0))
    value = pl.BlockSpec((parts, HEAD, size), lambda g: (0, g + KV_HEADS, 0))
    bias = pl.BlockSpec((parts * size, count), lambda g: (0, 0))
    log = pl.BlockSpec((1, 8, count), lambda g: (g, 0, 0))
    work = HEADS * count * parts * size
    return per_query, key, value, bias, log, work


def attend_forward(queries, both, bias):
    per_query, key, value, shared, log, work = attention_specs(queries, both)
    return pl.pallas_call(
        forward_kernel,
        grid=(KV_HEADS,),
        in_specs=[per_query, key, value, shared],
        out_specs=[per_query, log],
        out_shape=[
            jax.ShapeDtypeStruct(queries.shape, LOW),
            jax.ShapeDtypeStruct((KV_HEADS, 8, queries.shape[1]), jnp.float32),
        ],
        cost_estimate=pl.CostEstimate(
            flops=4 * HEAD * work, transcendentals=work, bytes_accessed=4 << 20
        ),
        name="attend_forward",
    )(queries, both, both, bias)


def attend_backward(queries, both, bias, mixed, log_norm, grad_mixed):
    per_query, key, value, shared, log, work = attention_specs(queries, both)
    parts, _, size = both.shape
    grad_kv = jax.ShapeDtypeStruct((parts, KV_HEADS * HEAD, size), jnp.float32)
    return pl.pallas_call(
        backward_kernel,
        grid=(KV_HEADS,),
        in_specs=[per_query, key, value, shared, per_query, log, per_query],
        out_specs=[per_query, key, key],
        out_shape=[jax.ShapeDtypeStruct(queries.shape, jnp.float32), grad_kv, grad_kv],
        cost_estimate=pl.CostEstimate(
            flops=10 * HEAD * work, transcendentals=work, bytes_accessed=8 << 20
        ),
        name="attend_backward",
    )(queries, both, both, bias, mixed, log_norm, grad_mixed)


def on_device(
    tokens,
    query_weight,
    key_weight,
    value_weight,
    out_weight,
    gate_weight,
    up_weight,
    down_weight,
    attention_gain,
    feedforward_gain,
    positions,
    segments,
    cotangent,
):
    row_index = lax.axis_index("rows")
    col_index = lax.axis_index("cols")
    dp_index = lax.axis_index("dp")
    dp_count = lax.axis_size("dp")
    row_count = lax.axis_size("rows")
    col_count = lax.axis_size("cols")
    feat_width, col_tokens = tokens.shape
    block_tokens = col_tokens // row_count
    half_block = block_tokens // 2
    layer_total = query_weight.shape[0]
    query_width = query_weight.shape[2]
    kv_width = key_weight.shape[2]
    all_queries = query_width * col_count
    all_kv = kv_width * col_count
    head_scale = HEAD ** (-0.5)

    deal = []
    for j in range(row_count):
        deal += [j, 2 * row_count - 1 - j]
    undeal = [deal.index(b) for b in range(2 * row_count)]

    def reorder(values, order):
        parts = [values[..., b * half_block : (b + 1) * half_block] for b in order]
        return jnp.concatenate(parts, -1)

    def to_token_blocks(values):
        chunks = spread(reorder(values, deal), row_count)
        return rows_exchange(chunks, row_index).reshape(-1, block_tokens).T

    def to_feature_blocks(values):
        chunks = values.astype(LOW).T.reshape(row_count, feat_width, block_tokens)
        return reorder(unspread(rows_exchange(chunks, row_index)), undeal).astype(jnp.float32)

    def blocks_here(values):
        dealt = reorder(values, deal).reshape(row_count, block_tokens)
        picked = [
            lax.dynamic_index_in_dim(dealt, row_index ^ i, 0, keepdims=False)
            for i in range(row_count)
        ]
        return jnp.concatenate(picked)

    places = blocks_here(jnp.arange(col_tokens, dtype=jnp.int32))
    own_positions = blocks_here(
        lax.dynamic_index_in_dim(positions, col_index, 0, keepdims=False)
    )[:block_tokens]
    doc = blocks_here(lax.dynamic_index_in_dim(segments, col_index, 0, keepdims=False))
    allowed = (places[:, None] <= places[None, :block_tokens]) & (
        doc[:, None] == doc[None, :block_tokens]
    )
    bias = jnp.where(allowed, 0.0, NEG_FILL)
    cosine, sine = rope_tables(own_positions)

    def attention_weights(layer):
        joint = jnp.concatenate(
            [query_weight[layer], key_weight[layer], value_weight[layer], out_weight[layer].T], 1
        )
        wide = lax.all_gather(joint, "cols", axis=0, tiled=True)
        wide = wide.reshape(col_count, feat_width, -1)
        ends = [query_width, query_width + kv_width, query_width + 2 * kv_width]
        parts = [unspread(part) for part in jnp.split(wide, ends, 2)]
        joint_full = lax.all_gather(
            jnp.concatenate(parts[:3], 1), "rows", axis=0, tiled=True
        )
        out_full = lax.all_gather(parts[3], "rows", axis=0, tiled=True)
        return joint_full, out_full

    def ffn_weights(layer):
        stacked = jnp.stack([gate_weight[layer], up_weight[layer], down_weight[layer]])
        chunks = stacked.transpose(0, 2, 1).reshape(3, row_count, 2, -1, feat_width)
        half = lax.dynamic_index_in_dim(chunks, dp_index % 2, 2, keepdims=False)
        whole = rows_exchange(half.transpose(1, 0, 2, 3), row_index)
        whole = whole.transpose(1, 2, 0, 3).reshape(-1, row_count * feat_width)
        own = lax.all_gather(whole, "cols", axis=0, tiled=True)
        other = swap_dp(own, 1)
        own = own.reshape(col_count, 3, -1, row_count * feat_width)
        other = other.reshape(own.shape)
        return [
            jnp.concatenate([own[:, i], other[:, i]], 0).reshape(-1, row_count * feat_width)
            for i in range(3)
        ]

    def attention_grads(joint_grad, out_grad):
        part = lax.psum_scatter(joint_grad.astype(LOW), "rows", scatter_dimension=0, tiled=True)
        out = lax.psum_scatter(out_grad.astype(LOW), "rows", scatter_dimension=0, tiled=True)
        ends = [all_queries, all_queries + all_kv]
        parts = [spread(p, col_count) for p in jnp.split(part, ends, 1) + [out]]
        joint = jnp.concatenate(parts, 2)
        joint = joint.reshape(col_count * feat_width, -1)
        joint = lax.psum_scatter(joint, "cols", scatter_dimension=0, tiled=True)
        step = 1
        while step < dp_count:
            joint = joint.astype(jnp.float32) + swap_dp(joint.astype(LOW), step).astype(jnp.float32)
            step *= 2
        ends = [query_width, query_width + kv_width, query_width + 2 * kv_width]
        parts = jnp.split(joint, ends, 1)
        return parts[0], parts[1], parts[2], parts[3].T

    def ffn_grads(grads):
        stacked = jnp.stack([g.astype(LOW).reshape(2, col_count, -1, g.shape[1]) for g in grads], 2)
        half = stacked[0].astype(jnp.float32) + swap_dp(stacked[1], 1).astype(jnp.float32)
        half = half.astype(LOW).reshape(-1, half.shape[-1])
        mine = lax.psum_scatter(half, "cols", scatter_dimension=0, tiled=True)
        step = 2
        while step < dp_count:
            mine = (mine.astype(jnp.float32) + swap_dp(mine, step).astype(jnp.float32)).astype(LOW)
            step *= 2
        chunks = mine.reshape(3, -1, row_count, feat_width).transpose(2, 0, 1, 3)
        mine = rows_exchange(chunks, row_index)
        other = swap_dp(mine, 1)
        first = dp_index % 2 == 0
        both = jnp.stack([jnp.where(first, mine, other), jnp.where(first, other, mine)], 2)
        both = both.transpose(1, 4, 0, 2, 3)
        return both.reshape(3, feat_width, -1).astype(jnp.float32)

    def everywhere(value):
        for axis in ("rows", "dp", "cols"):
            count = lax.axis_size(axis)
            step = 1
            while step < count:
                value = value + lax.ppermute(value, axis, [(i, i ^ step) for i in range(count)])
                step *= 2
        return value

    attention_ws = [attention_weights(n) for n in range(layer_total)]
    ffn_ws = [ffn_weights(n) for n in range(layer_total)]

    residual = to_token_blocks(tokens).astype(jnp.float32)
    saved = []
    for layer in range(layer_total):
        joint_full, out_full = attention_ws[layer]
        gate_full, up_full, down_full = ffn_ws[layer]
        normed, mixer_scale = norm_forward(residual, attention_gain[layer])
        projected = contract(joint_full, normed, 0, 1).astype(LOW).astype(jnp.float32)
        queries = (turn(projected[:all_queries], cosine, sine) * head_scale).astype(LOW)
        own_kv = jnp.concatenate(
            [
                turn(projected[all_queries : all_queries + all_kv], cosine, sine),
                projected[all_queries + all_kv :],
            ],
            0,
        ).astype(LOW)
        both = rows_gather(own_kv).reshape(row_count, 2 * all_kv, block_tokens)
        mixed, log_norm = attend_forward(queries, both, bias)
        hidden = residual + contract(mixed, out_full, 0, 1)
        ffn_normed, ffn_scale = norm_forward(hidden, feedforward_gain[layer])
        ffn_all = rows_gather(ffn_normed)
        gate = contract(ffn_all, gate_full, 1, 1)
        up = contract(ffn_all, up_full, 1, 1)
        activated = (gate * jax.nn.sigmoid(gate) * up).astype(LOW)
        ffn_out = rows_scatter(contract(activated, down_full, 1, 0))
        saved.append(
            (residual, mixer_scale, normed, queries, both, log_norm, mixed, hidden)
            + (ffn_scale, ffn_all, gate, up, activated)
        )
        residual = hidden + ffn_out

    weight_grads = [None] * layer_total
    gain_grads = [None] * layer_total
    grad = to_token_blocks(cotangent).astype(jnp.float32)
    for layer in reversed(range(layer_total)):
        joint_full, out_full = attention_ws[layer]
        gate_full, up_full, down_full = ffn_ws[layer]
        layer_input, mixer_scale, normed, queries, both, log_norm, mixed, hidden = saved[layer][:8]
        ffn_scale, ffn_all, gate, up, activated = saved[layer][8:]
        grad_all = rows_gather(grad.astype(LOW))
        grad_act = contract(grad_all, down_full, 1, 1)
        down_grad = contract(activated, grad_all, 0, 0)
        sig = jax.nn.sigmoid(gate)
        grad_gate = (grad_act * up * sig * (1.0 + gate * (1.0 - sig))).astype(LOW)
        grad_up = (grad_act * gate * sig).astype(LOW)
        grad_ffn_normed = rows_scatter(
            contract(grad_gate, gate_full, 1, 0) + contract(grad_up, up_full, 1, 0)
        )
        gate_grad = contract(grad_gate, ffn_all, 0, 0)
        up_grad = contract(grad_up, ffn_all, 0, 0)
        ffn_norm_grad, ffn_gain_grad = norm_backward(
            grad_ffn_normed, hidden, ffn_scale, feedforward_gain[layer]
        )
        grad_hidden = grad + ffn_norm_grad
        grad_low = grad_hidden.astype(LOW)
        grad_mixed = contract(out_full, grad_low, 0, 1).astype(LOW)
        out_grad = contract(grad_low, mixed, 0, 1)
        grad_query, grad_key, grad_value = attend_backward(
            queries, both, bias, mixed, log_norm, grad_mixed
        )
        grad_kv = jnp.concatenate([grad_key, grad_value], 1).reshape(-1, block_tokens)
        grad_kv = rows_scatter(grad_kv)
        grad_joint = jnp.concatenate(
            [
                turn(grad_query, cosine, -sine) * head_scale,
                turn(grad_kv[:all_kv], cosine, -sine),
                grad_kv[all_kv:],
            ],
            0,
        ).astype(LOW)
        grad_normed = contract(grad_joint, joint_full, 0, 1)
        joint_grad = contract(normed, grad_joint, 0, 1)
        mixer_norm_grad, mixer_gain_grad = norm_backward(
            grad_normed, layer_input, mixer_scale, attention_gain[layer]
        )
        grad = grad_hidden + mixer_norm_grad
        ffn_parts = ffn_grads([gate_grad, up_grad, down_grad])
        weight_grads[layer] = attention_grads(joint_grad, out_grad) + (
            ffn_parts[0],
            ffn_parts[1],
            ffn_parts[2],
        )
        gain_grads[layer] = jnp.stack([mixer_gain_grad, ffn_gain_grad])

    gain_total = everywhere(jnp.stack(gain_grads))
    totals = [jnp.stack([weight_grads[n][i] for n in range(layer_total)]) for i in range(7)]
    return (
        to_feature_blocks(residual),
        to_feature_blocks(grad),
        totals[0],
        totals[1],
        totals[2],
        totals[3],
        totals[4],
        totals[5],
        totals[6],
        gain_total[:, 0],
        gain_total[:, 1],
    )


def solution(mesh):
    whole = P("rows", ("dp", "cols"))
    weight = P(None, "rows", "cols")
    flipped = P(None, "cols", "rows")
    return jax.shard_map(
        on_device,
        mesh=mesh,
        in_specs=(whole, weight, weight, weight, flipped, weight, weight, weight)
        + (P(), P(), P("dp", None), P("dp", None), whole),
        out_specs=(whole, whole, weight, weight, weight, flipped, weight, weight, weight, P(), P()),
        check_vma=False,
    )
```

time: 885 us -> 788 us (0.89)
  matrix products: 208 us -> 88 us
  blocking collectives: 120 us -> 0 us
  Pallas kernels: 0 us -> 71 us
  waiting for transfers between devices: 297 us -> 340 us
  local copies, waits for them, and re-layouts: 121 us -> 158 us
  other arithmetic: 71.1 us -> 58.6 us
    dot_general x70 -> x0, matrix products: 106 us -> none  [the longest x20 22.2 us: one_group(): jnp.einsum('gqd,kd->gqk', query_set, key_set, preferred_element_type=jnp....]
    all_gather x4 -> x0, blocking collectives: 79.3 us -> none  [the longest x2 41.6 us: attention_weights(): wide = lax.all_gather(joint, 'cols', axis=0)]
    pallas_call x0 -> x4, Pallas kernels: none -> 71 us  [the longest x2 39.8 us: attend_backward(): pl.pallas_call(backward_kernel, grid=(KV_HEADS,), in_specs=[per_query, ke...]
    ppermute x6 -> x13, waiting for transfers between devices: 46 us -> 108 us  [the longest x8 104 us: swap_dp(): return lax.ppermute(value, 'dp', [(i, i ^ step) for i in range(count)])]
    psum x1 -> x0, blocking collectives: 40.5 us -> none  [on_device(): gain_total = lax.psum(jnp.stack(gain_grads), ('dp', 'rows', 'cols'))]
    reduce_scatter x10 -> x4, waiting for transfers between devices: 34.3 us -> 0.06 us  [the longest x2 0.04 us: ffn_grads(): mine = lax.psum_scatter(half, 'cols', scatter_dimension=0, tiled=True)]
    all_gather x10 -> x8, waiting for transfers between devices: 44 us -> 73.4 us  [the longest x2 32.6 us: attention_weights(): wide = lax.all_gather(joint, 'cols', axis=0, tiled=True)]
    convert_element_type x0 -> x8, local copies, waits for them, and re-layouts: none -> 17.5 us  [the longest x6 14.5 us: ffn_grads(): g.astype(LOW).reshape(2, col_count, -1, g.shape[1])]
  transfers between devices with their start and end apart: 78 -> 77, of which waited for: 33 -> 36; matrix products, arithmetic and copies ran while one was open for 42% -> 33% of each run, Pallas kernels for 0% -> 9%
where the time goes in v2:
time: 788 us; the launch traced here: 777 us
  waiting for transfers between devices  340 us (43%)
  local copies, waits for them, and re-layouts  158 us (20%)
  matrix products  88 us (11%)
  Pallas kernels  71 us (9%)
  other arithmetic  58.6 us (7%)
  starting transfers between devices  44.6 us (6%)
  between operations  17.3 us (2%)
    ppermute x48, waiting for transfers between devices, swap_rows(): return lax.ppermute(value, 'rows', [(i, i ^ step) for i in range(count)])  158 us
    ppermute x8, waiting for transfers between devices, swap_dp(): return lax.ppermute(value, 'dp', [(i, i ^ step) for i in range(count)])  104 us
    dot_general x30, matrix products, contract(): lax.dot_general(left, right, (((left_dim,), (right_dim,)), ((), ())), pre...  88 us
    unnamed x282, local copies, waits for them, and re-layouts  46.6 us
    pallas_call x2, Pallas kernels, attend_backward(): pl.pallas_call(backward_kernel, grid=(KV_HEADS,), in_specs=[per_query, ke...  39.8 us
    all_gather x2, waiting for transfers between devices, attention_weights(): wide = lax.all_gather(joint, 'cols', axis=0, tiled=True)  32.6 us
    pallas_call x2, Pallas kernels, attend_forward(): pl.pallas_call(forward_kernel, grid=(KV_HEADS,), in_specs=[per_query, key...  31.2 us
    all_gather x2, waiting for transfers between devices, ffn_weights(): own = lax.all_gather(whole, 'cols', axis=0, tiled=True)  28.6 us
  transfers between devices with their start and end apart: 77, of which 36 were waited for; matrix products, arithmetic and copies ran while one was open for 33% of the time, Pallas kernels for 9%

profile of v2, /device:TPU:0, one launch (start us, length us, event | category | flops | bytes accessed | tf_op | source)
XLA Modules:
  0.0 777.3 jit_solution(6795934616791013260)
XLA Ops:
  13.4 32.6 %all-gather.9.cloned.1.call-done = bf16[960,640]{1,0:T(8,128)(2,1)} async-done(((bf16[240,640]{1,0:T(8,128)(2,1)}), bf16[960,640]{1,0:T(8,128)(2,1)}) %all-gather.9.cloned.1.call-update) | async-done | bytes 1228816 | tf_op jit(solution)/shard_map/all_gather | solution.py:280
  100.9 7.8 %all-gather.11.cloned.1.call-done = bf16[960,1600]{1,0:T(8,128)(2,1)} async-done(((bf16[240,1600]{1,0:T(8,128)(2,1)}), bf16[960,1600]{1,0:T(8,128)(2,1)}) %all-gather.11.cloned.1.call-update) | async-done | bytes 3072016 | tf_op jit(solution)/shard_map/all_gather | solution.py:284
  108.8 3.2 convolution_convert_fusion.3
  113.9 9.5 %collective-permute-done.3 = bf16[640,256]{1,0:T(8,128)(2,1)S(1)} collective-permute-done((bf16[640,256]{1,0:T(8,128)(2,1)S(1)}, bf16[640,256]{1,0:T(8,128)(2,1)S(1)}, u32[]{:S(2)}, u32[]{:S(2)}) %collective-permute-start.3) | collective-permute-done | bytes 327712 | tf_op jit(solution)/shard_map/ppermute | solution.py:33
  125.7 28.6 %all-gather.15.cloned.1.call-done = bf16[960,960]{1,0:T(8,128)(2,1)} async-done(((bf16[240,960]{1,0:T(8,128)(2,1)}), bf16[960,960]{1,0:T(8,128)(2,1)}) %all-gather.15.cloned.1.call-update) | async-done | bytes 1843216 | tf_op jit(solution)/shard_map/all_gather | solution.py:296
  161.0 11.5 %attend_forward.2 = (bf16[960,256]{1,0:T(8,128)(2,1)}, f32[5,8,256]{2,1,0:T(8,128)}) custom-call(bf16[960,256]{1,0:T(8,128)(2,1)} %bitcast.570, bf16[4,640,256]{2,1,0:T(8,128)(2,1)} %bitcast.29.key_ref.value_ref, bf16[4,640,256]{2,1,0:T(8,128)(2,1)} %bitcast.29.key_ref.value_ref, f32[1024,256]{1,0:T(8,128)} %and_select_fusion.bias_ref), custom_call_target="tpu_custom_call" | custom-call | flops 1006632960 | bytes 4194304 | tf_op jit(solution)/shard_map/attend_forward/pallas_call | solution.py:176
  172.6 4.3 all-gather.13.cloned.1.call-done
  183.2 15.3 %collective-permute-done.5 = bf16[256,960]{0,1:T(8,128)(2,1)S(1)} collective-permute-done((bf16[256,960]{0,1:T(8,128)(2,1)S(1)}, bf16[256,960]{0,1:T(8,128)(2,1)S(1)}, u32[]{:S(2)}, u32[]{:S(2)}) %collective-permute-start.5) | collective-permute-done | bytes 491552 | tf_op jit(solution)/shard_map/ppermute | solution.py:33
  210.5 3.9 multiply_convert_fusion.5
  226.7 7.9 %collective-permute-done.12 = bf16[256,960]{0,1:T(8,128)(2,1)} collective-permute-done((bf16[256,960]{0,1:T(8,128)(2,1)}, bf16[256,960]{0,1:T(8,128)(2,1)}, u32[]{:S(2)}, u32[]{:S(2)}) %collective-permute-start.12) | collective-permute-done | bytes 491552 | tf_op jit(solution)/shard_map/ppermute | solution.py:33
  236.5 3.2 convolution_convert_fusion.2
  245.4 6.6 collective-permute-done.13
  253.0 7.5 collective-permute-done.29
  270.2 19.6 %attend_forward.3 = (bf16[960,256]{1,0:T(8,128)(2,1)}, f32[5,8,256]{2,1,0:T(8,128)}) custom-call(bf16[960,256]{1,0:T(8,128)(2,1)} %bitcast.572, bf16[4,640,256]{2,1,0:T(8,128)(2,1)} %bitcast.85.key_ref.value_ref, bf16[4,640,256]{2,1,0:T(8,128)(2,1)} %bitcast.85.key_ref.value_ref, f32[1024,256]{1,0:T(8,128)} %and_select_fusion.bias_ref), custom_call_target="tpu_custom_call" | custom-call | flops 1006632960 | bytes 4194304 | tf_op jit(solution)/shard_map/attend_forward/pallas_call | solution.py:176
  292.9 12.9 %collective-permute-done.15 = bf16[256,960]{0,1:T(8,128)(2,1)S(1)} collective-permute-done((bf16[256,960]{0,1:T(8,128)(2,1)S(1)}, bf16[256,960]{0,1:T(8,128)(2,1)S(1)}, u32[]{:S(2)}, u32[]{:S(2)}) %collective-permute-start.15) | collective-permute-done | bytes 491552 | tf_op jit(solution)/shard_map/ppermute | solution.py:33
  314.0 4.8 multiply_convert_fusion.2
  319.9 2.7 convolution_convert_fusion.6
  325.1 4.6 convolution_convert_fusion.8
  332.4 4.6 convolution_convert_fusion.7
  345.4 3.7 fusion.95
  351.1 3.8 fusion.96
  356.0 30.9 %collective-permute-done.51 = bf16[4,3,80,960]{3,2,0,1:T(8,128)(2,1)S(1)} collective-permute-done((bf16[4,3,80,960]{3,2,0,1:T(8,128)(2,1)S(1)}, bf16[4,3,80,960]{3,2,0,1:T(8,128)(2,1)S(1)}, u32[]{:S(2)}, u32[]{:S(2)}) %collective-permute-start.51) | collective-permute-done | bytes 1843232 | tf_op jit(solution)/shard_map/ppermute | solution.py:79
  394.6 10.5 %collective-permute-done.32 = bf16[256,960]{0,1:T(8,128)(2,1)S(1)} collective-permute-done((bf16[256,960]{0,1:T(8,128)(2,1)S(1)}, bf16[256,960]{0,1:T(8,128)(2,1)S(1)}, u32[]{:S(2)}, u32[]{:S(2)}) %collective-permute-start.32) | collective-permute-done | bytes 491552 | tf_op jit(solution)/shard_map/ppermute | solution.py:33
  406.8 7.1 collective-permute-done.22
  413.9 2.9 subtract_add_fusion.2
  418.3 20.1 %attend_backward.2 = (f32[960,256]{1,0:T(8,128)}, f32[4,320,256]{2,1,0:T(8,128)}, f32[4,320,256]{2,1,0:T(8,128)}) custom-call(bf16[960,256]{1,0:T(8,128)(2,1)} %bitcast.573, bf16[4,640,256]{2,1,0:T(8,128)(2,1)} %bitcast.85.key_ref.value_ref, bf16[4,640,256]{2,1,0:T(8,128)(2,1)} %bitcast.85.key_ref.value_ref, f32[1024,256]{1,0:T(8,128)} %and_select_fusion.bias_ref, ...), custom_call_target="tpu_custom_call" | custom-call | flops 2516582400 | bytes 8388608 | tf_op jit(solution)/shard_map/attend_backward/pallas_call | solution.py:196
  447.7 8.6 %collective-permute-done.34 = bf16[640,256]{1,0:T(8,128)(2,1)S(1)} collective-permute-done((bf16[640,256]{1,0:T(8,128)(2,1)S(1)}, bf16[640,256]{1,0:T(8,128)(2,1)S(1)}, u32[]{:S(2)}, u32[]{:S(2)}) %collective-permute-start.34) | collective-permute-done | bytes 327712 | tf_op jit(solution)/shard_map/ppermute | solution.py:33
  460.7 22.0 %collective-permute-done.35 = bf16[256,960]{0,1:T(8,128)(2,1)S(1)} collective-permute-done((bf16[256,960]{0,1:T(8,128)(2,1)S(1)}, bf16[256,960]{0,1:T(8,128)(2,1)S(1)}, u32[]{:S(2)}, u32[]{:S(2)}) %collective-permute-start.35) | collective-permute-done | bytes 491552 | tf_op jit(solution)/shard_map/ppermute | solution.py:33
  483.9 2.9 convolution_convert_fusion
  488.6 5.3 multiply_convert_fusion
  503.0 2.7 convolution_convert_fusion.9
  507.3 19.1 %collective-permute-done.38 = bf16[256,960]{0,1:T(8,128)(2,1)} collective-permute-done((bf16[256,960]{0,1:T(8,128)(2,1)}, bf16[256,960]{0,1:T(8,128)(2,1)}, u32[]{:S(2)}, u32[]{:S(2)}) %collective-permute-start.38) | collective-permute-done | bytes 491552 | tf_op jit(solution)/shard_map/ppermute | solution.py:33
  532.4 4.3 convolution_convert_fusion.11
  536.7 2.7 copy.217
  539.4 4.3 convolution_convert_fusion.10
  548.5 43.4 %collective-permute-done.46 = bf16[4,3,80,960]{3,2,0,1:T(8,128)(2,1)S(1)} collective-permute-done((bf16[4,3,80,960]{3,2,0,1:T(8,128)(2,1)S(1)}, bf16[4,3,80,960]{3,2,0,1:T(8,128)(2,1)S(1)}, u32[]{:S(2)}, u32[]{:S(2)}) %collective-permute-start.46) | collective-permute-done | bytes 1843232 | tf_op jit(solution)/shard_map/ppermute | solution.py:79
  594.4 3.1 convolution_convert_fusion.12.grad_ref
  597.5 19.7 %attend_backward.3 = (f32[960,256]{1,0:T(8,128)}, f32[4,320,256]{2,1,0:T(8,128)}, f32[4,320,256]{2,1,0:T(8,128)}) custom-call(bf16[960,256]{1,0:T(8,128)(2,1)} %bitcast.571, bf16[4,640,256]{2,1,0:T(8,128)(2,1)} %bitcast.29.key_ref.value_ref, bf16[4,640,256]{2,1,0:T(8,128)(2,1)} %bitcast.29.key_ref.value_ref, f32[1024,256]{1,0:T(8,128)} %and_select_fusion.bias_ref, ...), custom_call_target="tpu_custom_call" | custom-call | flops 2516582400 | bytes 8388608 | tf_op jit(solution)/shard_map/attend_backward/pallas_call | solution.py:196
  623.9 7.7 collective-permute-done.40
  631.9 2.8 convolution_convert_fusion.1
  637.8 4.4 collective-permute-done.24
  649.1 4.1 collective-permute-done.53
  657.7 10.7 %collective-permute-done.55 = bf16[4,3,80,240]{3,2,1,0:T(8,128)(2,1)} collective-permute-done((bf16[4,3,80,240]{3,2,1,0:T(8,128)(2,1)S(1)}, bf16[4,3,80,240]{3,2,1,0:T(8,128)(2,1)}, u32[]{:S(2)}, u32[]{:S(2)}) %collective-permute-start.55) | collective-permute-done | bytes 460832 | tf_op jit(solution)/shard_map/ppermute | solution.py:79
  669.5 4.0 fusion.30
  692.1 2.8 pad_maximum_fusion.16
  705.6 4.3 collective-permute-done.42
  732.9 11.0 %collective-permute-done.50 = bf16[4,3,80,240]{3,2,1,0:T(8,128)(2,1)S(1)} collective-permute-done((bf16[4,3,80,240]{3,2,1,0:T(8,128)(2,1)S(1)}, bf16[4,3,80,240]{3,2,1,0:T(8,128)(2,1)S(1)}, u32[]{:S(2)}, u32[]{:S(2)}) %collective-permute-start.50) | collective-permute-done | bytes 460832 | tf_op jit(solution)/shard_map/ppermute | solution.py:79
  758.9 6.7 collective-permute-done.44
  (716 shorter events, 293.1 us)
Async XLA Ops:
  7.2 38.9 %all-gather.9.cloned.1.call-start = ((), (), s32[]{:S(2)}) async-start(), calls=%async_computation.8 | async-start | bytes 1536000 | tf_op jit(solution)/shard_map/all_gather | solution.py:280
  12.1 82.9 %all-gather.17.cloned.1.call-start = ((), (), s32[]{:S(2)}) async-start(), calls=%async_computation.12 | async-start | bytes 1536000 | tf_op jit(solution)/shard_map/all_gather | solution.py:280
  13.4 95.4 %all-gather.11.cloned.1.call-start = ((), (), s32[]{:S(2)}) async-start(), calls=%async_computation.9 | async-start | bytes 3993600 | tf_op jit(solution)/shard_map/all_gather | solution.py:284
  50.9 103.3 %all-gather.15.cloned.1.call-start = ((), (), s32[]{:S(2)}) async-start(), calls=%async_computation.11 | async-start | bytes 2457600 | tf_op jit(solution)/shard_map/all_gather | solution.py:296
  53.9 36.8 %collective-permute-start = (bf16[1,240,256]{2,1,0:T(8,128)(2,1)}, bf16[1,240,256]{2,1,0:T(8,128)(2,1)}, u32[]{:S(2)}, u32[]{:S(2)}) collective-permute-start(bf16[1,240,256]{2,1,0:T(8,128)(2,1)} %bitcast.469), channel_id=1, source_target_pairs={{0,4},{4,0},{8,12},{12,8},{1,5},{5,1},{9,13},{13,9},{2,6},{6,2},{1... | collective-permute-start | bytes 368648 | tf_op jit(solution)/shard_map/ppermute | solution.py:33
  54.6 37.7 %collective-permute-start.1 = (bf16[1,240,256]{2,1,0:T(8,128)(2,1)}, bf16[1,240,256]{2,1,0:T(8,128)(2,1)}, u32[]{:S(2)}, u32[]{:S(2)}) collective-permute-start(bf16[1,240,256]{2,1,0:T(8,128)(2,1)} %bitcast.468), channel_id=1, source_target_pairs={{0,8},{4,12},{8,0},{12,4},{1,9},{5,13},{9,1},{13,5},{2,10},{6,14},... | collective-permute-start | bytes 368648 | tf_op jit(solution)/shard_map/ppermute | solution.py:33
  56.1 37.1 %collective-permute-start.2 = (bf16[1,240,256]{2,1,0:T(8,128)(2,1)S(1)}, bf16[1,240,256]{2,1,0:T(8,128)(2,1)}, u32[]{:S(2)}, u32[]{:S(2)}) collective-permute-start(bf16[1,240,256]{2,1,0:T(8,128)(2,1)S(1)} %bitcast.588), channel_id=1, source_target_pairs={{0,12},{4,8},{8,4},{12,0},{1,13},{5,9},{9,5},{13,1},{2,14},{6,10},... | collective-permute-start | bytes 368648 | tf_op jit(solution)/shard_map/ppermute | solution.py:33
  69.9 129.7 %collective-permute-start.19 = (bf16[1,3,80,240]{3,2,1,0:T(8,128)(2,1)}, bf16[1,3,80,240]{3,2,1,0:T(8,128)(2,1)}, u32[]{:S(2)}, u32[]{:S(2)}) collective-permute-start(bf16[1,3,80,240]{3,2,1,0:T(8,128)(2,1)} %get-tuple-element.150), channel_id=1, source_target_pairs={{0,12},{4,8},{8,4},{12,0},{1,13},{5,9},{9,5},{13,1},{2,14},{6,10},... | collective-permute-start | bytes 345608 | tf_op jit(solution)/shard_map/ppermute | solution.py:33
  73.3 109.0 %collective-permute-start.18 = (bf16[1,3,80,240]{3,2,1,0:T(8,128)(2,1)}, bf16[1,3,80,240]{3,2,1,0:T(8,128)(2,1)}, u32[]{:S(2)}, u32[]{:S(2)}) collective-permute-start(bf16[1,3,80,240]{3,2,1,0:T(8,128)(2,1)} %get-tuple-element.151), channel_id=1, source_target_pairs={{0,8},{4,12},{8,0},{12,4},{1,9},{5,13},{9,1},{13,5},{2,10},{6,14},... | collective-permute-start | bytes 345608 | tf_op jit(solution)/shard_map/ppermute | solution.py:33
  75.7 101.2 %all-gather.13.cloned.1.call-start = ((), (), s32[]{:S(2)}) async-start(), calls=%async_computation.10 | async-start | bytes 2457600 | tf_op jit(solution)/shard_map/all_gather | solution.py:287
  86.9 149.6 %all-gather.19.cloned.1.call-start = ((), (), s32[]{:S(2)}) async-start(), calls=%async_computation.13 | async-start | bytes 3993600 | tf_op jit(solution)/shard_map/all_gather | solution.py:284
  90.7 90.7 %collective-permute-start.17 = (bf16[1,3,80,240]{3,2,1,0:T(8,128)(2,1)}, bf16[1,3,80,240]{3,2,1,0:T(8,128)(2,1)}, u32[]{:S(2)}, u32[]{:S(2)}) collective-permute-start(bf16[1,3,80,240]{3,2,1,0:T(8,128)(2,1)} %get-tuple-element.152), channel_id=1, source_target_pairs={{0,4},{4,0},{8,12},{12,8},{1,5},{5,1},{9,13},{13,9},{2,6},{6,2},{1... | collective-permute-start | bytes 345608 | tf_op jit(solution)/shard_map/ppermute | solution.py:33
  100.6 161.7 %all-gather.23.cloned.1.call-start = ((), (), s32[]{:S(2)}) async-start(), calls=%async_computation.15 | async-start | bytes 2457600 | tf_op jit(solution)/shard_map/all_gather | solution.py:296
  124.3 32.5 %collective-permute-start.4 = (bf16[1280,256]{1,0:T(8,128)(2,1)}, bf16[1280,256]{1,0:T(8,128)(2,1)}, u32[]{:S(2)}, u32[]{:S(2)}) collective-permute-start(bf16[1280,256]{1,0:T(8,128)(2,1)} %pad_maximum_fusion.31), channel_id=1, source_target_pairs={{0,4},{4,0},{8,12},{12,8},{1,5},{5,1},{9,13},{13,9},{2,6},{6,2},{1... | collective-permute-start | bytes 1966088 | tf_op jit(solution)/shard_map/ppermute | solution.py:33
  154.2 49.7 %collective-permute-start.10 = (bf16[960,960]{1,0:T(8,128)(2,1)}, bf16[960,960]{1,0:T(8,128)(2,1)}, u32[]{:S(2)}, u32[]{:S(2)}) collective-permute-start(bf16[960,960]{1,0:T(8,128)(2,1)} %all-gather.15.cloned.1.call-done), channel_id=1, source_target_pairs={{0,16},{16,0},{1,17},{17,1},{2,18},{18,2},{3,19},{19,3},{4,20},{20... | collective-permute-start | bytes 5529608 | tf_op jit(solution)/shard_map/ppermute | solution.py:79
  180.0 18.5 %collective-permute-start.5 = (bf16[256,960]{0,1:T(8,128)(2,1)S(1)}, bf16[256,960]{0,1:T(8,128)(2,1)S(1)}, u32[]{:S(2)}, u32[]{:S(2)}) collective-permute-start(bf16[256,960]{0,1:T(8,128)(2,1)S(1)} %multiply_convert_fusion.8), channel_id=1, source_target_pairs={{0,8},{4,12},{8,0},{12,4},{1,9},{5,13},{9,1},{13,5},{2,10},{6,14},... | collective-permute-start | bytes 1474568 | tf_op jit(solution)/shard_map/ppermute | solution.py:33
  202.1 87.7 %all-gather.21.cloned.1.call-start = ((), (), s32[]{:S(2)}) async-start(), calls=%async_computation.14 | async-start | bytes 2457600 | tf_op jit(solution)/shard_map/all_gather | solution.py:287
  220.3 14.4 %collective-permute-start.12 = (bf16[256,960]{0,1:T(8,128)(2,1)}, bf16[256,960]{0,1:T(8,128)(2,1)}, u32[]{:S(2)}, u32[]{:S(2)}) collective-permute-start(bf16[256,960]{0,1:T(8,128)(2,1)} %fusion.10), channel_id=1, source_target_pairs={{0,8},{4,12},{8,0},{12,4},{1,9},{5,13},{9,1},{13,5},{2,10},{6,14},... | collective-permute-start | bytes 1474568 | tf_op jit(solution)/shard_map/ppermute | solution.py:33
  222.9 18.9 %collective-permute-start.27 = (bf16[1,240,256]{2,1,0:T(8,128)(2,1)}, bf16[1,240,256]{2,1,0:T(8,128)(2,1)}, u32[]{:S(2)}, u32[]{:S(2)}) collective-permute-start(bf16[1,240,256]{2,1,0:T(8,128)(2,1)} %bitcast.465), channel_id=1, source_target_pairs={{0,8},{4,12},{8,0},{12,4},{1,9},{5,13},{9,1},{13,5},{2,10},{6,14},... | collective-permute-start | bytes 368648 | tf_op jit(solution)/shard_map/ppermute | solution.py:33
  225.2 17.5 %collective-permute-start.28 = (bf16[1,240,256]{2,1,0:T(8,128)(2,1)}, bf16[1,240,256]{2,1,0:T(8,128)(2,1)}, u32[]{:S(2)}, u32[]{:S(2)}) collective-permute-start(bf16[1,240,256]{2,1,0:T(8,128)(2,1)} %bitcast.464), channel_id=1, source_target_pairs={{0,12},{4,8},{8,4},{12,0},{1,13},{5,9},{9,5},{13,1},{2,14},{6,10},... | collective-permute-start | bytes 368648 | tf_op jit(solution)/shard_map/ppermute | solution.py:33
  226.7 417.3 %reduce-scatter.23.cloned.1.call-start = ((), (), s32[]{:S(2)}) async-start(), calls=%async_computation.23 | async-start | bytes 2457600 | tf_op jit(solution)/shard_map/reduce_scatter | solution.py:325
  241.4 10.6 %collective-permute-start.13 = (bf16[640,256]{1,0:T(8,128)(2,1)S(1)}, bf16[640,256]{1,0:T(8,128)(2,1)S(1)}, u32[]{:S(2)}, u32[]{:S(2)}) collective-permute-start(bf16[640,256]{1,0:T(8,128)(2,1)S(1)} %pad_maximum_fusion.46), channel_id=1, source_target_pairs={{0,8},{4,12},{8,0},{12,4},{1,9},{5,13},{9,1},{13,5},{2,10},{6,14},... | collective-permute-start | bytes 983048 | tf_op jit(solution)/shard_map/ppermute | solution.py:33
  243.7 16.9 %collective-permute-start.29 = (bf16[256,960]{0,1:T(8,128)(2,1)S(1)}, bf16[256,960]{0,1:T(8,128)(2,1)S(1)}, u32[]{:S(2)}, u32[]{:S(2)}) collective-permute-start(bf16[256,960]{0,1:T(8,128)(2,1)S(1)} %bitcast.492), channel_id=1, source_target_pairs={{0,8},{4,12},{8,0},{12,4},{1,9},{5,13},{9,1},{13,5},{2,10},{6,14},... | collective-permute-start | bytes 1474568 | tf_op jit(solution)/shard_map/ppermute | solution.py:33
  253.0 13.1 %collective-permute-start.14 = (bf16[1280,256]{1,0:T(8,128)(2,1)}, bf16[1280,256]{1,0:T(8,128)(2,1)}, u32[]{:S(2)}, u32[]{:S(2)}) collective-permute-start(bf16[1280,256]{1,0:T(8,128)(2,1)} %pad_maximum_fusion.32), channel_id=1, source_target_pairs={{0,4},{4,0},{8,12},{12,8},{1,5},{5,1},{9,13},{13,9},{2,6},{6,2},{1... | collective-permute-start | bytes 1966088 | tf_op jit(solution)/shard_map/ppermute | solution.py:33
  262.3 43.6 %collective-permute-start.30 = (bf16[512,960]{0,1:T(8,128)(2,1)}, bf16[512,960]{0,1:T(8,128)(2,1)}, u32[]{:S(2)}, u32[]{:S(2)}) collective-permute-start(bf16[512,960]{0,1:T(8,128)(2,1)} %pad_maximum_fusion.23), channel_id=1, source_target_pairs={{0,4},{4,0},{8,12},{12,8},{1,5},{5,1},{9,13},{13,9},{2,6},{6,2},{1... | collective-permute-start | bytes 2949128 | tf_op jit(solution)/shard_map/ppermute | solution.py:33
  262.4 45.5 %collective-permute-start.20 = (bf16[960,960]{1,0:T(8,128)(2,1)}, bf16[960,960]{1,0:T(8,128)(2,1)}, u32[]{:S(2)}, u32[]{:S(2)}) collective-permute-start(bf16[960,960]{1,0:T(8,128)(2,1)} %all-gather.23.cloned.1.call-done), channel_id=1, source_target_pairs={{0,16},{16,0},{1,17},{17,1},{2,18},{18,2},{3,19},{19,3},{4,20},{20... | collective-permute-start | bytes 5529608 | tf_op jit(solution)/shard_map/ppermute | solution.py:79
  292.4 13.4 %collective-permute-start.15 = (bf16[256,960]{0,1:T(8,128)(2,1)S(1)}, bf16[256,960]{0,1:T(8,128)(2,1)S(1)}, u32[]{:S(2)}, u32[]{:S(2)}) collective-permute-start(bf16[256,960]{0,1:T(8,128)(2,1)S(1)} %multiply_convert_fusion.6), channel_id=1, source_target_pairs={{0,8},{4,12},{8,0},{12,4},{1,9},{5,13},{9,1},{13,5},{2,10},{6,14},... | collective-permute-start | bytes 1474568 | tf_op jit(solution)/shard_map/ppermute | solution.py:33
  342.1 44.8 %collective-permute-start.51 = (bf16[4,3,80,960]{3,2,0,1:T(8,128)(2,1)S(1)}, bf16[4,3,80,960]{3,2,0,1:T(8,128)(2,1)S(1)}, u32[]{:S(2)}, u32[]{:S(2)}) collective-permute-start(bf16[4,3,80,960]{3,2,0,1:T(8,128)(2,1)S(1)} %slice_bitcast_fusion), channel_id=1, source_target_pairs={{0,16},{16,0},{1,17},{17,1},{2,18},{18,2},{3,19},{19,3},{4,20},{20... | collective-permute-start | bytes 5529608 | tf_op jit(solution)/shard_map/ppermute | solution.py:79
  350.2 39.2 %collective-permute-start.31 = (bf16[512,960]{0,1:T(8,128)(2,1)}, bf16[512,960]{0,1:T(8,128)(2,1)}, u32[]{:S(2)}, u32[]{:S(2)}) collective-permute-start(bf16[512,960]{0,1:T(8,128)(2,1)} %pad_maximum_fusion.24), channel_id=1, source_target_pairs={{0,4},{4,0},{8,12},{12,8},{1,5},{5,1},{9,13},{13,9},{2,6},{6,2},{1... | collective-permute-start | bytes 2949128 | tf_op jit(solution)/shard_map/ppermute | solution.py:33
  356.0 35.6 %collective-permute-start.21 = (bf16[512,960]{0,1:T(8,128)(2,1)}, bf16[512,960]{0,1:T(8,128)(2,1)}, u32[]{:S(2)}, u32[]{:S(2)}) collective-permute-start(bf16[512,960]{0,1:T(8,128)(2,1)} %pad_maximum_fusion.22), channel_id=1, source_target_pairs={{0,4},{4,0},{8,12},{12,8},{1,5},{5,1},{9,13},{13,9},{2,6},{6,2},{1... | collective-permute-start | bytes 2949128 | tf_op jit(solution)/shard_map/ppermute | solution.py:33
  389.3 266.7 %reduce-scatter.17.cloned.1.call-start = ((), (), s32[]{:S(2)}) async-start(), calls=%async_computation.20 | async-start | bytes 2457600 | tf_op jit(solution)/shard_map/reduce_scatter | solution.py:307
  391.0 14.2 %collective-permute-start.32 = (bf16[256,960]{0,1:T(8,128)(2,1)S(1)}, bf16[256,960]{0,1:T(8,128)(2,1)S(1)}, u32[]{:S(2)}, u32[]{:S(2)}) collective-permute-start(bf16[256,960]{0,1:T(8,128)(2,1)S(1)} %fusion.4), channel_id=1, source_target_pairs={{0,8},{4,12},{8,0},{12,4},{1,9},{5,13},{9,1},{13,5},{2,10},{6,14},... | collective-permute-start | bytes 1474568 | tf_op jit(solution)/shard_map/ppermute | solution.py:33
  393.0 20.8 %collective-permute-start.22 = (bf16[256,960]{0,1:T(8,128)(2,1)S(1)}, bf16[256,960]{0,1:T(8,128)(2,1)S(1)}, u32[]{:S(2)}, u32[]{:S(2)}) collective-permute-start(bf16[256,960]{0,1:T(8,128)(2,1)S(1)} %fusion.6), channel_id=1, source_target_pairs={{0,8},{4,12},{8,0},{12,4},{1,9},{5,13},{9,1},{13,5},{2,10},{6,14},... | collective-permute-start | bytes 1474568 | tf_op jit(solution)/shard_map/ppermute | solution.py:33
  445.3 233.7 %reduce-scatter.15.cloned.1.call-start = ((), (), s32[]{:S(2)}) async-start(), calls=%async_computation.19 | async-start | bytes 3993600 | tf_op jit(solution)/shard_map/reduce_scatter | solution.py:306
  460.1 22.7 %collective-permute-start.35 = (bf16[256,960]{0,1:T(8,128)(2,1)S(1)}, bf16[256,960]{0,1:T(8,128)(2,1)S(1)}, u32[]{:S(2)}, u32[]{:S(2)}) collective-permute-start(bf16[256,960]{0,1:T(8,128)(2,1)S(1)} %get-tuple-element.83), channel_id=1, source_target_pairs={{0,8},{4,12},{8,0},{12,4},{1,9},{5,13},{9,1},{13,5},{2,10},{6,14},... | collective-permute-start | bytes 1474568 | tf_op jit(solution)/shard_map/ppermute | solution.py:33
  486.8 223.4 %reduce-scatter.11.cloned.1.call-start = ((), (), s32[]{:S(2)}) async-start(), calls=%async_computation.17 | async-start | bytes 2457600 | tf_op jit(solution)/shard_map/reduce_scatter | solution.py:307
  502.2 24.3 %collective-permute-start.38 = (bf16[256,960]{0,1:T(8,128)(2,1)}, bf16[256,960]{0,1:T(8,128)(2,1)}, u32[]{:S(2)}, u32[]{:S(2)}) collective-permute-start(bf16[256,960]{0,1:T(8,128)(2,1)} %fusion.2), channel_id=1, source_target_pairs={{0,8},{4,12},{8,0},{12,4},{1,9},{5,13},{9,1},{13,5},{2,10},{6,14},... | collective-permute-start | bytes 1474568 | tf_op jit(solution)/shard_map/ppermute | solution.py:33
  532.3 180.2 %reduce-scatter.21.cloned.1.call-start = ((), (), s32[]{:S(2)}) async-start(), calls=%async_computation.22 | async-start | bytes 2457600 | tf_op jit(solution)/shard_map/reduce_scatter | solution.py:325
  548.4 43.5 %collective-permute-start.46 = (bf16[4,3,80,960]{3,2,0,1:T(8,128)(2,1)S(1)}, bf16[4,3,80,960]{3,2,0,1:T(8,128)(2,1)S(1)}, u32[]{:S(2)}, u32[]{:S(2)}) collective-permute-start(bf16[4,3,80,960]{3,2,0,1:T(8,128)(2,1)S(1)} %slice_bitcast_fusion.2), channel_id=1, source_target_pairs={{0,16},{16,0},{1,17},{17,1},{2,18},{18,2},{3,19},{19,3},{4,20},{20... | collective-permute-start | bytes 5529608 | tf_op jit(solution)/shard_map/ppermute | solution.py:79
  594.3 124.6 %reduce-scatter.9.cloned.1.call-start = ((), (), s32[]{:S(2)}) async-start(), calls=%async_computation.16 | async-start | bytes 3993600 | tf_op jit(solution)/shard_map/reduce_scatter | solution.py:306
  634.8 111.6 %reduce-scatter.19.cloned.1.call-start = ((), (), s32[]{:S(2)}) async-start(), calls=%async_computation.21 | async-start | bytes 1536000 | tf_op jit(solution)/shard_map/reduce_scatter | solution.py:312
  654.7 13.8 %collective-permute-start.55 = (bf16[4,3,80,240]{3,2,1,0:T(8,128)(2,1)S(1)}, bf16[4,3,80,240]{3,2,1,0:T(8,128)(2,1)}, u32[]{:S(2)}, u32[]{:S(2)}) collective-permute-start(bf16[4,3,80,240]{3,2,1,0:T(8,128)(2,1)S(1)} %constant_dynamic-update-slice_fusion.37), channel_id=1, source_target_pairs={{0,16},{16,0},{1,17},{17,1},{2,18},{18,2},{3,19},{19,3},{4,20},{20... | collective-permute-start | bytes 1382408 | tf_op jit(solution)/shard_map/ppermute | solution.py:79
  678.7 16.6 %collective-permute-start.58 = (f32[2,2,960]{2,0,1:T(2,128)S(1)}, f32[2,2,960]{2,0,1:T(2,128)}, u32[]{:S(2)}, u32[]{:S(2)}) collective-permute-start(f32[2,2,960]{2,0,1:T(2,128)S(1)} %fusion.136), channel_id=1, source_target_pairs={{0,16},{16,0},{1,17},{17,1},{2,18},{18,2},{3,19},{19,3},{4,20},{20... | collective-permute-start | bytes 46088 | tf_op jit(solution)/shard_map/ppermute | solution.py:343
  694.9 62.0 %reduce-scatter.13.cloned.1.call-start = ((), (), s32[]{:S(2)}) async-start(), calls=%async_computation.18 | async-start | bytes 1536000 | tf_op jit(solution)/shard_map/reduce_scatter | solution.py:312
  717.0 10.2 %collective-permute-start.47 = (bf16[1,3,80,240]{3,2,1,0:T(8,128)(2,1)}, bf16[1,3,80,240]{3,2,1,0:T(8,128)(2,1)}, u32[]{:S(2)}, u32[]{:S(2)}) collective-permute-start(bf16[1,3,80,240]{3,2,1,0:T(8,128)(2,1)} %bitcast.463), channel_id=1, source_target_pairs={{0,4},{4,0},{8,12},{12,8},{1,5},{5,1},{9,13},{13,9},{2,6},{6,2},{1... | collective-permute-start | bytes 345608 | tf_op jit(solution)/shard_map/ppermute | solution.py:33
  717.5 10.7 %collective-permute-start.48 = (bf16[1,3,80,240]{3,2,1,0:T(8,128)(2,1)}, bf16[1,3,80,240]{3,2,1,0:T(8,128)(2,1)}, u32[]{:S(2)}, u32[]{:S(2)}) collective-permute-start(bf16[1,3,80,240]{3,2,1,0:T(8,128)(2,1)} %bitcast.462), channel_id=1, source_target_pairs={{0,8},{4,12},{8,0},{12,4},{1,9},{5,13},{9,1},{13,5},{2,10},{6,14},... | collective-permute-start | bytes 345608 | tf_op jit(solution)/shard_map/ppermute | solution.py:33
  718.2 10.9 %collective-permute-start.49 = (bf16[1,3,80,240]{3,2,1,0:T(8,128)(2,1)}, bf16[1,3,80,240]{3,2,1,0:T(8,128)(2,1)}, u32[]{:S(2)}, u32[]{:S(2)}) collective-permute-start(bf16[1,3,80,240]{3,2,1,0:T(8,128)(2,1)} %bitcast.461), channel_id=1, source_target_pairs={{0,12},{4,8},{8,4},{12,0},{1,13},{5,9},{9,5},{13,1},{2,14},{6,10},... | collective-permute-start | bytes 345608 | tf_op jit(solution)/shard_map/ppermute | solution.py:33
  730.0 13.9 %collective-permute-start.50 = (bf16[4,3,80,240]{3,2,1,0:T(8,128)(2,1)S(1)}, bf16[4,3,80,240]{3,2,1,0:T(8,128)(2,1)S(1)}, u32[]{:S(2)}, u32[]{:S(2)}) collective-permute-start(bf16[4,3,80,240]{3,2,1,0:T(8,128)(2,1)S(1)} %constant_dynamic-update-slice_fusion.40), channel_id=1, source_target_pairs={{0,16},{16,0},{1,17},{17,1},{2,18},{18,2},{3,19},{19,3},{4,20},{20... | collective-permute-start | bytes 1382408 | tf_op jit(solution)/shard_map/ppermute | solution.py:79
  (129 other events, 905.5 us)
Sparse Core Ops, SparseCore 0:
  12.2 33.8 all-gather.8
  48.2 30.2 all-gather.16
  80.7 28.0 all-gather.10
  110.8 43.4 all-gather.14
  156.2 20.6 all-gather.12
  178.9 33.1 all-gather.18
  213.7 43.4 all-gather.22
  258.8 20.6 all-gather.20
  389.5 41.2 reduce-scatter.22
  445.4 38.5 reduce-scatter.16
  486.9 47.4 reduce-scatter.14
  536.8 29.5 reduce-scatter.10
  594.5 40.9 reduce-scatter.20
  637.8 37.2 reduce-scatter.8
  695.0 30.3 reduce-scatter.18
  727.6 29.0 reduce-scatter.12
